TPU v7x, 512 devices: a whole 4x4x16 slice. The times are simulated.
512 devices in a mesh: slab: 32 (over z, y_lo), face: 16 (over y_hi, x, core).
Axes of the slice: x: 4, y: 4 (y_hi: 2, y_lo: 2; y = y_hi * 2 + y_lo), z: 16, core: 2. Of those that a mesh axis runs over, the one named last changes fastest.
Arguments:
- rhs: bfloat16 [4, 32, 128, 16384], P(None, 'slab', None, 'face'), may hold values from -6 to 6
- inflow: bfloat16 [32, 128, 4096], P('slab', None, 'face'), may hold values from -6 to 6
- diag_tiles: bfloat16 [32, 128, 128, 128], P('slab', 'face')
- off_tiles: bfloat16 [32, 128, 4, 128, 128], P('slab', 'face'), may hold values from -0.5 to 0.5
- cols: int32 [32, 128, 4], P('slab', 'face'), may hold values from 0 to 127, as said below
- inverse_tiles: bfloat16 [32, 128, 128, 128], P('slab', 'face')
- coupling: bfloat16 [32, 32, 128, 128], P('slab', 'face'), may hold values from -1 to 1
- iface: int32 [32], P('face'), may hold values from 0 to 7, as said below
Outputs:
- solution: bfloat16 [4, 32, 128, 16384], P(None, 'slab', None, 'face')
Inputs may be any that keep to these rules, and one draw needn't show every extreme that they name: `cols`: each column index lies within 2 tile rows of the block of 8 tile rows that holds its row; a block's first tile row reaches the tile row 2 before the block and its last reaches the tile row 2 after the block, wherever the slab has them. The 2 entries of one block of iface are distinct.
All inputs are finite; a program needn't handle non-finite values.
Results may differ from a plain program's by a relative error of at most 0.01.
Values may be sent and summed in bfloat16 or wider, within the bound.
A program may use at most 64 MiB of HBM per device.

v0:
```python
import jax
import jax.numpy as jnp
from jax import lax
from jax.sharding import PartitionSpec as P

HALO_T = 2


def padded(value, sides, width):
    for axis, dim in sides:
        size, length = (lax.axis_size(axis), value.shape[dim])
        up = [(i, (i + 1) % size) for i in range(size - 1)]
        down = [(j, i) for i, j in up]
        last = lax.slice_in_dim(value, length - width, length, axis=dim)
        leading = lax.slice_in_dim(value, 0, width, axis=dim)
        before = lax.ppermute(last, axis, up)
        after = lax.ppermute(leading, axis, down)
        value = jnp.concatenate([before, value, after], axis=dim)
    return value


def from_behind(block, axis, distance):
    devices = range(lax.axis_size(axis))
    route = [(i - distance, i) for i in devices if i - distance in devices]
    return lax.ppermute(block, axis, route)


def tile_apply(tiles, values):
    return jnp.einsum("rij,srj->sri", tiles, values, preferred_element_type=jnp.float32)


def on_device(rhs, inflow, diag_tiles, off_tiles, cols, inverse_tiles, coupling, iface):
    face_index = lax.axis_index("face")
    diagonal = diag_tiles[0]
    neighbours = off_tiles[0]
    inverse = inverse_tiles[0]
    couple = coupling[0]
    count = diagonal.shape[0]
    width = diagonal.shape[1]
    iface_count = couple.shape[0]
    local_cols = cols[0] - (face_index * count - HALO_T)
    selector = (iface[None, :] == jnp.arange(count, dtype=jnp.int32)[:, None]).astype(jnp.float32)
    rhs_local = rhs[:, 0]
    inflow_local = inflow[0]
    incoming = inflow_local
    results = []
    total = rhs_local.shape[0]
    for tick in range(total):
        rhs_tick = rhs_local[tick]
        sources = rhs_tick.shape[0]
        inbound = incoming.reshape(sources, iface_count, width)
        coupled = jnp.einsum("qij,sqj->sqi", couple, inbound, preferred_element_type=jnp.float32)
        placed = jnp.einsum("rq,sqi->sri", selector, coupled)
        right = (rhs_tick.reshape(sources, count, width).astype(jnp.float32) - placed).astype(
            jnp.bfloat16
        )
        advance_field = tile_apply(inverse, right).astype(jnp.bfloat16)
        for sweep in range(2):
            extended = padded(advance_field, (("face", 1),), HALO_T)
            gathered = jnp.take(extended, local_cols, axis=1)
            product = tile_apply(diagonal, advance_field) + jnp.einsum(
                "rkij,srkj->sri", neighbours, gathered, preferred_element_type=jnp.float32
            )
            correction = (right.astype(jnp.float32) - product).astype(jnp.bfloat16)
            advance_field = (
                advance_field.astype(jnp.float32) + tile_apply(inverse, correction)
            ).astype(jnp.bfloat16)
        sent = jnp.take(advance_field, iface, axis=1).reshape(sources, iface_count * width)
        field, sent = (advance_field.reshape(sources, count * width), sent)
        results.append(field)
        if tick + 1 < total:
            incoming = from_behind(sent, "slab", 1)
    solution = jnp.stack(results)
    return solution[:, None]


def solution(mesh):
    placed = (
        P(None, "slab", None, "face"),
        P("slab", None, "face"),
        P("slab", "face", None, None),
        P("slab", "face", None, None, None),
        P("slab", "face", None),
        P("slab", "face", None, None),
        P("slab", "face", None, None),
        P("face"),
    )
    return jax.shard_map(
        on_device,
        mesh=mesh,
        in_specs=placed,
        out_specs=P(None, "slab", None, "face"),
        check_vma=False,
    )
```

profile of v0, /device:TPU:400, one launch (start us, length us, event | category | flops | bytes accessed | tf_op | source)
XLA Modules:
  0.0 168.1 jit_solution(14022958141891491245)
XLA Ops:
  0.0 2.6 %convert_bitcast_fusion.3 = (f32[16,8,8,128]{3,1,2,0:T(8,128)S(1)}, f32[16,8,8,128]{3,1,2,0:T(8,128)}, f32[16,8,8,128]{3,1,2,0:T(8,128)}, f32[16,8,8,128]{3,1,2,0:T(8,128)}) fusion(bf16[4,1,128,1024]{3,2,1,0:T(8,128)(2,1)} %param.12), kind=kLoop, calls=%fused_computation.131 | loop fusion | flops 524288 | bytes 3145728
  2.7 0.7 copy-done.14
  3.4 0.8 copy-done.8
  4.4 0.7 copy-done.15
  6.4 4.0 %collective-permute-start.1 = (bf16[128,2,128]{0,2,1:T(8,128)(2,1)S(1)}, bf16[128,2,128]{0,2,1:T(8,128)(2,1)S(1)}, u32[]{:S(2)}, u32[]{:S(2)}) collective-permute-start(bf16[128,2,128]{0,2,1:T(8,128)(2,1)S(1)} %get-tuple-element.28), channel_id=1, source_target_pairs={{1,0},{2,1},{3,2},{4,3},{5,4},{6,5},{7,6},{8,7},{9,8},{10,9},{11,1... | collective-permute-start | bytes 196616 | tf_op jit(solution)/shard_map/ppermute | solution.py:17
  10.4 1.9 %collective-permute-start = (bf16[128,2,128]{0,2,1:T(8,128)(2,1)S(1)}, bf16[128,2,128]{0,2,1:T(8,128)(2,1)S(1)}, u32[]{:S(2)}, u32[]{:S(2)}) collective-permute-start(bf16[128,2,128]{0,2,1:T(8,128)(2,1)S(1)} %get-tuple-element.27), channel_id=1, source_target_pairs={{0,1},{1,2},{2,3},{3,4},{4,5},{5,6},{6,7},{7,8},{8,9},{9,10},{10,1... | collective-permute-start | bytes 196616 | tf_op jit(solution)/shard_map/ppermute | solution.py:16
  12.3 0.7 copy-done.16
  13.7 5.9 %collective-permute-done = bf16[128,2,128]{0,2,1:T(8,128)(2,1)S(1)} collective-permute-done((bf16[128,2,128]{0,2,1:T(8,128)(2,1)S(1)}, bf16[128,2,128]{0,2,1:T(8,128)(2,1)S(1)}, u32[]{:S(2)}, u32[]{:S(2)}) %collective-permute-start) | collective-permute-done | bytes 65568 | tf_op jit(solution)/shard_map/ppermute | solution.py:16
  19.6 1.7 gather_fusion
  21.3 1.8 %fusion.49 = f32[8,128,128,1]{2,1,3,0:T(8,128)S(1)} fusion(bf16[1,8,4,128,128]{4,3,2,1,0:T(8,128)(2,1)S(1)} %copy-done, bf16[8,4,128,128]{2,3,1,0:T(8,128)(2,1)} %bitcast.309, pred[8,4]{1,0:T(8,128)(4,1)S(1)} %copy.42), kind=kOutput, calls=%fused_computation.77 | convolution fusion | flops 134742016 | bytes 2621472 | tf_op jit(solution)/shard_map/rkij,srkj->sri/dot_general | solution.py:61
  23.1 0.6 fusion.68
  24.0 1.9 %collective-permute-start.3 = (bf16[128,2,128]{0,2,1:T(8,128)(2,1)S(1)}, bf16[128,2,128]{0,2,1:T(8,128)(2,1)S(1)}, u32[]{:S(2)}, u32[]{:S(2)}) collective-permute-start(bf16[128,2,128]{0,2,1:T(8,128)(2,1)S(1)} %get-tuple-element.26), channel_id=1, source_target_pairs={{1,0},{2,1},{3,2},{4,3},{5,4},{6,5},{7,6},{8,7},{9,8},{10,9},{11,1... | collective-permute-start | bytes 196616 | tf_op jit(solution)/shard_map/ppermute | solution.py:17
  25.9 2.4 %collective-permute-start.2 = (bf16[128,2,128]{0,2,1:T(8,128)(2,1)S(1)}, bf16[128,2,128]{0,2,1:T(8,128)(2,1)S(1)}, u32[]{:S(2)}, u32[]{:S(2)}) collective-permute-start(bf16[128,2,128]{0,2,1:T(8,128)(2,1)S(1)} %get-tuple-element.25), channel_id=1, source_target_pairs={{0,1},{1,2},{2,3},{3,4},{4,5},{5,6},{6,7},{7,8},{8,9},{9,10},{10,1... | collective-permute-start | bytes 196616 | tf_op jit(solution)/shard_map/ppermute | solution.py:16
  28.7 6.5 %collective-permute-done.2 = bf16[128,2,128]{0,2,1:T(8,128)(2,1)S(1)} collective-permute-done((bf16[128,2,128]{0,2,1:T(8,128)(2,1)S(1)}, bf16[128,2,128]{0,2,1:T(8,128)(2,1)S(1)}, u32[]{:S(2)}, u32[]{:S(2)}) %collective-permute-start.2) | collective-permute-done | bytes 65568 | tf_op jit(solution)/shard_map/ppermute | solution.py:16
  35.2 1.7 gather_fusion.1
  36.9 1.8 %fusion.40 = f32[8,128,128,1]{2,1,3,0:T(8,128)S(1)} fusion(bf16[1,8,4,128,128]{4,3,2,1,0:T(8,128)(2,1)S(1)} %copy-done, bf16[8,4,128,128]{2,3,1,0:T(8,128)(2,1)} %bitcast.310, pred[8,4]{1,0:T(8,128)(4,1)S(1)} %copy.42), kind=kOutput, calls=%fused_computation.68 | convolution fusion | flops 134742016 | bytes 2621472 | tf_op jit(solution)/shard_map/rkij,srkj->sri/dot_general | solution.py:61
  38.7 0.6 fusion.69
  40.2 4.1 %collective-permute-start.4 = (bf16[128,256]{0,1:T(8,128)(2,1)S(1)}, bf16[128,256]{0,1:T(8,128)(2,1)S(1)}, u32[]{:S(2)}, u32[]{:S(2)}) collective-permute-start(bf16[128,256]{0,1:T(8,128)(2,1)S(1)} %bitcast.321), channel_id=1, source_target_pairs={{0,16},{16,32},{32,48},{48,64},{64,80},{80,96},{96,112},{112,128},... | collective-permute-start | bytes 196616 | tf_op jit(solution)/shard_map/ppermute | solution.py:25
  44.5 4.3 %collective-permute-done.4 = bf16[128,256]{0,1:T(8,128)(2,1)S(1)} collective-permute-done((bf16[128,256]{0,1:T(8,128)(2,1)S(1)}, bf16[128,256]{0,1:T(8,128)(2,1)S(1)}, u32[]{:S(2)}, u32[]{:S(2)}) %collective-permute-start.4) | collective-permute-done | bytes 65568 | tf_op jit(solution)/shard_map/ppermute | solution.py:25
  49.7 1.9 %collective-permute-start.6 = (bf16[128,2,128]{0,2,1:T(8,128)(2,1)S(1)}, bf16[128,2,128]{0,2,1:T(8,128)(2,1)S(1)}, u32[]{:S(2)}, u32[]{:S(2)}) collective-permute-start(bf16[128,2,128]{0,2,1:T(8,128)(2,1)S(1)} %get-tuple-element.24), channel_id=1, source_target_pairs={{1,0},{2,1},{3,2},{4,3},{5,4},{6,5},{7,6},{8,7},{9,8},{10,9},{11,1... | collective-permute-start | bytes 196616 | tf_op jit(solution)/shard_map/ppermute | solution.py:17
  51.6 2.4 %collective-permute-start.5 = (bf16[128,2,128]{0,2,1:T(8,128)(2,1)S(1)}, bf16[128,2,128]{0,2,1:T(8,128)(2,1)S(1)}, u32[]{:S(2)}, u32[]{:S(2)}) collective-permute-start(bf16[128,2,128]{0,2,1:T(8,128)(2,1)S(1)} %get-tuple-element.23), channel_id=1, source_target_pairs={{0,1},{1,2},{2,3},{3,4},{4,5},{5,6},{6,7},{7,8},{8,9},{9,10},{10,1... | collective-permute-start | bytes 196616 | tf_op jit(solution)/shard_map/ppermute | solution.py:16
  54.4 6.5 %collective-permute-done.5 = bf16[128,2,128]{0,2,1:T(8,128)(2,1)S(1)} collective-permute-done((bf16[128,2,128]{0,2,1:T(8,128)(2,1)S(1)}, bf16[128,2,128]{0,2,1:T(8,128)(2,1)S(1)}, u32[]{:S(2)}, u32[]{:S(2)}) %collective-permute-start.5) | collective-permute-done | bytes 65568 | tf_op jit(solution)/shard_map/ppermute | solution.py:16
  60.9 1.7 gather_fusion.3
  62.6 0.7 copy-done.18
  63.2 1.8 %fusion.38 = f32[8,128,128,1]{2,1,3,0:T(8,128)S(1)} fusion(bf16[1,8,4,128,128]{4,3,2,1,0:T(8,128)(2,1)S(1)} %copy-done, bf16[8,4,128,128]{2,3,1,0:T(8,128)(2,1)} %bitcast.311, pred[8,4]{1,0:T(8,128)(4,1)S(1)} %copy-done.18), kind=kOutput, calls=%fused_computation.66 | convolution fusion | flops 134742016 | bytes 2621472 | tf_op jit(solution)/shard_map/rkij,srkj->sri/dot_general | solution.py:61
  65.0 0.6 fusion.70
  65.9 1.9 %collective-permute-start.8 = (bf16[128,2,128]{0,2,1:T(8,128)(2,1)S(1)}, bf16[128,2,128]{0,2,1:T(8,128)(2,1)S(1)}, u32[]{:S(2)}, u32[]{:S(2)}) collective-permute-start(bf16[128,2,128]{0,2,1:T(8,128)(2,1)S(1)} %get-tuple-element.22), channel_id=1, source_target_pairs={{1,0},{2,1},{3,2},{4,3},{5,4},{6,5},{7,6},{8,7},{9,8},{10,9},{11,1... | collective-permute-start | bytes 196616 | tf_op jit(solution)/shard_map/ppermute | solution.py:17
  67.9 2.4 %collective-permute-start.7 = (bf16[128,2,128]{0,2,1:T(8,128)(2,1)S(1)}, bf16[128,2,128]{0,2,1:T(8,128)(2,1)S(1)}, u32[]{:S(2)}, u32[]{:S(2)}) collective-permute-start(bf16[128,2,128]{0,2,1:T(8,128)(2,1)S(1)} %get-tuple-element.21), channel_id=1, source_target_pairs={{0,1},{1,2},{2,3},{3,4},{4,5},{5,6},{6,7},{7,8},{8,9},{9,10},{10,1... | collective-permute-start | bytes 196616 | tf_op jit(solution)/shard_map/ppermute | solution.py:16
  70.6 6.5 %collective-permute-done.7 = bf16[128,2,128]{0,2,1:T(8,128)(2,1)S(1)} collective-permute-done((bf16[128,2,128]{0,2,1:T(8,128)(2,1)S(1)}, bf16[128,2,128]{0,2,1:T(8,128)(2,1)S(1)}, u32[]{:S(2)}, u32[]{:S(2)}) %collective-permute-start.7) | collective-permute-done | bytes 65568 | tf_op jit(solution)/shard_map/ppermute | solution.py:16
  77.1 1.7 gather_fusion.4
  78.8 0.7 copy-done.19
  79.5 1.8 %fusion.36 = f32[8,128,128,1]{2,1,3,0:T(8,128)S(1)} fusion(bf16[1,8,4,128,128]{4,3,2,1,0:T(8,128)(2,1)S(1)} %copy-done, bf16[8,4,128,128]{2,3,1,0:T(8,128)(2,1)} %bitcast.312, pred[8,4]{1,0:T(8,128)(4,1)S(1)} %copy-done.19), kind=kOutput, calls=%fused_computation.64 | convolution fusion | flops 134742016 | bytes 2621472 | tf_op jit(solution)/shard_map/rkij,srkj->sri/dot_general | solution.py:61
  82.8 1.9 %collective-permute-start.9 = (bf16[128,256]{0,1:T(8,128)(2,1)S(1)}, bf16[128,256]{0,1:T(8,128)(2,1)S(1)}, u32[]{:S(2)}, u32[]{:S(2)}) collective-permute-start(bf16[128,256]{0,1:T(8,128)(2,1)S(1)} %bitcast.322), channel_id=1, source_target_pairs={{0,16},{16,32},{32,48},{48,64},{64,80},{80,96},{96,112},{112,128},... | collective-permute-start | bytes 196616 | tf_op jit(solution)/shard_map/ppermute | solution.py:25
  84.9 6.2 %collective-permute-done.9 = bf16[128,256]{0,1:T(8,128)(2,1)S(1)} collective-permute-done((bf16[128,256]{0,1:T(8,128)(2,1)S(1)}, bf16[128,256]{0,1:T(8,128)(2,1)S(1)}, u32[]{:S(2)}, u32[]{:S(2)}) %collective-permute-start.9) | collective-permute-done | bytes 65568 | tf_op jit(solution)/shard_map/ppermute | solution.py:25
  92.0 1.9 %collective-permute-start.11 = (bf16[128,2,128]{0,2,1:T(8,128)(2,1)S(1)}, bf16[128,2,128]{0,2,1:T(8,128)(2,1)S(1)}, u32[]{:S(2)}, u32[]{:S(2)}) collective-permute-start(bf16[128,2,128]{0,2,1:T(8,128)(2,1)S(1)} %get-tuple-element.20), channel_id=1, source_target_pairs={{1,0},{2,1},{3,2},{4,3},{5,4},{6,5},{7,6},{8,7},{9,8},{10,9},{11,1... | collective-permute-start | bytes 196616 | tf_op jit(solution)/shard_map/ppermute | solution.py:17
  93.9 2.4 %collective-permute-start.10 = (bf16[128,2,128]{0,2,1:T(8,128)(2,1)S(1)}, bf16[128,2,128]{0,2,1:T(8,128)(2,1)S(1)}, u32[]{:S(2)}, u32[]{:S(2)}) collective-permute-start(bf16[128,2,128]{0,2,1:T(8,128)(2,1)S(1)} %get-tuple-element.19), channel_id=1, source_target_pairs={{0,1},{1,2},{2,3},{3,4},{4,5},{5,6},{6,7},{7,8},{8,9},{9,10},{10,1... | collective-permute-start | bytes 196616 | tf_op jit(solution)/shard_map/ppermute | solution.py:16
  96.6 6.5 %collective-permute-done.10 = bf16[128,2,128]{0,2,1:T(8,128)(2,1)S(1)} collective-permute-done((bf16[128,2,128]{0,2,1:T(8,128)(2,1)S(1)}, bf16[128,2,128]{0,2,1:T(8,128)(2,1)S(1)}, u32[]{:S(2)}, u32[]{:S(2)}) %collective-permute-start.10) | collective-permute-done | bytes 65568 | tf_op jit(solution)/shard_map/ppermute | solution.py:16
  103.2 1.7 gather_fusion.6
  104.8 0.7 copy-done.20
  105.5 1.8 %fusion.34 = f32[8,128,128,1]{2,1,3,0:T(8,128)S(1)} fusion(bf16[1,8,4,128,128]{4,3,2,1,0:T(8,128)(2,1)S(1)} %copy-done, bf16[8,4,128,128]{2,3,1,0:T(8,128)(2,1)} %bitcast.313, pred[8,4]{1,0:T(8,128)(4,1)S(1)} %copy-done.20), kind=kOutput, calls=%fused_computation.62 | convolution fusion | flops 134742016 | bytes 2621472 | tf_op jit(solution)/shard_map/rkij,srkj->sri/dot_general | solution.py:61
  108.2 1.9 %collective-permute-start.13 = (bf16[128,2,128]{0,2,1:T(8,128)(2,1)S(1)}, bf16[128,2,128]{0,2,1:T(8,128)(2,1)S(1)}, u32[]{:S(2)}, u32[]{:S(2)}) collective-permute-start(bf16[128,2,128]{0,2,1:T(8,128)(2,1)S(1)} %get-tuple-element.18), channel_id=1, source_target_pairs={{1,0},{2,1},{3,2},{4,3},{5,4},{6,5},{7,6},{8,7},{9,8},{10,9},{11,1... | collective-permute-start | bytes 196616 | tf_op jit(solution)/shard_map/ppermute | solution.py:17
  110.1 2.6 %collective-permute-start.12 = (bf16[128,2,128]{0,2,1:T(8,128)(2,1)S(1)}, bf16[128,2,128]{0,2,1:T(8,128)(2,1)S(1)}, u32[]{:S(2)}, u32[]{:S(2)}) collective-permute-start(bf16[128,2,128]{0,2,1:T(8,128)(2,1)S(1)} %get-tuple-element.17), channel_id=1, source_target_pairs={{0,1},{1,2},{2,3},{3,4},{4,5},{5,6},{6,7},{7,8},{8,9},{9,10},{10,1... | collective-permute-start | bytes 196616 | tf_op jit(solution)/shard_map/ppermute | solution.py:16
  113.0 6.3 %collective-permute-done.12 = bf16[128,2,128]{0,2,1:T(8,128)(2,1)S(1)} collective-permute-done((bf16[128,2,128]{0,2,1:T(8,128)(2,1)S(1)}, bf16[128,2,128]{0,2,1:T(8,128)(2,1)S(1)}, u32[]{:S(2)}, u32[]{:S(2)}) %collective-permute-start.12) | collective-permute-done | bytes 65568 | tf_op jit(solution)/shard_map/ppermute | solution.py:16
  119.4 1.7 gather_fusion.7
  121.0 0.7 copy-done.21
  121.7 1.8 %fusion.32 = f32[8,128,128,1]{2,1,3,0:T(8,128)S(1)} fusion(bf16[1,8,4,128,128]{4,3,2,1,0:T(8,128)(2,1)S(1)} %copy-done, bf16[8,4,128,128]{2,3,1,0:T(8,128)(2,1)} %bitcast.314, pred[8,4]{1,0:T(8,128)(4,1)S(1)} %copy-done.21), kind=kOutput, calls=%fused_computation.60 | convolution fusion | flops 134742016 | bytes 2621472 | tf_op jit(solution)/shard_map/rkij,srkj->sri/dot_general | solution.py:61
  125.0 1.9 %collective-permute-start.14 = (bf16[128,256]{0,1:T(8,128)(2,1)S(1)}, bf16[128,256]{0,1:T(8,128)(2,1)S(1)}, u32[]{:S(2)}, u32[]{:S(2)}) collective-permute-start(bf16[128,256]{0,1:T(8,128)(2,1)S(1)} %bitcast.320), channel_id=1, source_target_pairs={{0,16},{16,32},{32,48},{48,64},{64,80},{80,96},{96,112},{112,128},... | collective-permute-start | bytes 196616 | tf_op jit(solution)/shard_map/ppermute | solution.py:25
  127.2 0.8 copy-done.7
  128.0 0.8 copy.70
  128.9 0.8 copy.71
  129.7 3.6 %collective-permute-done.14 = bf16[128,256]{0,1:T(8,128)(2,1)S(1)} collective-permute-done((bf16[128,256]{0,1:T(8,128)(2,1)S(1)}, bf16[128,256]{0,1:T(8,128)(2,1)S(1)}, u32[]{:S(2)}, u32[]{:S(2)}) %collective-permute-start.14) | collective-permute-done | bytes 65568 | tf_op jit(solution)/shard_map/ppermute | solution.py:25
  134.2 1.9 %collective-permute-start.16 = (bf16[128,2,128]{0,2,1:T(8,128)(2,1)S(1)}, bf16[128,2,128]{0,2,1:T(8,128)(2,1)S(1)}, u32[]{:S(2)}, u32[]{:S(2)}) collective-permute-start(bf16[128,2,128]{0,2,1:T(8,128)(2,1)S(1)} %get-tuple-element.16), channel_id=1, source_target_pairs={{1,0},{2,1},{3,2},{4,3},{5,4},{6,5},{7,6},{8,7},{9,8},{10,9},{11,1... | collective-permute-start | bytes 196616 | tf_op jit(solution)/shard_map/ppermute | solution.py:17
  136.1 2.4 %collective-permute-start.15 = (bf16[128,2,128]{0,2,1:T(8,128)(2,1)S(1)}, bf16[128,2,128]{0,2,1:T(8,128)(2,1)S(1)}, u32[]{:S(2)}, u32[]{:S(2)}) collective-permute-start(bf16[128,2,128]{0,2,1:T(8,128)(2,1)S(1)} %get-tuple-element.15), channel_id=1, source_target_pairs={{0,1},{1,2},{2,3},{3,4},{4,5},{5,6},{6,7},{7,8},{8,9},{9,10},{10,1... | collective-permute-start | bytes 196616 | tf_op jit(solution)/shard_map/ppermute | solution.py:16
  138.9 6.4 %collective-permute-done.15 = bf16[128,2,128]{0,2,1:T(8,128)(2,1)S(1)} collective-permute-done((bf16[128,2,128]{0,2,1:T(8,128)(2,1)S(1)}, bf16[128,2,128]{0,2,1:T(8,128)(2,1)S(1)}, u32[]{:S(2)}, u32[]{:S(2)}) %collective-permute-start.15) | collective-permute-done | bytes 65568 | tf_op jit(solution)/shard_map/ppermute | solution.py:16
  145.4 1.7 gather_fusion.9
  147.0 0.7 copy-done.22
  147.7 1.8 %fusion.30 = f32[8,128,128,1]{2,1,3,0:T(8,128)S(1)} fusion(bf16[1,8,4,128,128]{4,3,2,1,0:T(8,128)(2,1)S(1)} %copy-done, bf16[8,4,128,128]{2,3,1,0:T(8,128)(2,1)} %bitcast.315, pred[8,4]{1,0:T(8,128)(4,1)S(1)} %copy-done.22), kind=kOutput, calls=%fused_computation.58 | convolution fusion | flops 134742016 | bytes 2621472 | tf_op jit(solution)/shard_map/rkij,srkj->sri/dot_general | solution.py:61
  150.4 1.9 %collective-permute-start.18 = (bf16[128,2,128]{0,2,1:T(8,128)(2,1)S(1)}, bf16[128,2,128]{0,2,1:T(8,128)(2,1)S(1)}, u32[]{:S(2)}, u32[]{:S(2)}) collective-permute-start(bf16[128,2,128]{0,2,1:T(8,128)(2,1)S(1)} %get-tuple-element.14), channel_id=1, source_target_pairs={{1,0},{2,1},{3,2},{4,3},{5,4},{6,5},{7,6},{8,7},{9,8},{10,9},{11,1... | collective-permute-start | bytes 196616 | tf_op jit(solution)/shard_map/ppermute | solution.py:17
  152.3 2.4 %collective-permute-start.17 = (bf16[128,2,128]{0,2,1:T(8,128)(2,1)S(1)}, bf16[128,2,128]{0,2,1:T(8,128)(2,1)S(1)}, u32[]{:S(2)}, u32[]{:S(2)}) collective-permute-start(bf16[128,2,128]{0,2,1:T(8,128)(2,1)S(1)} %get-tuple-element.13), channel_id=1, source_target_pairs={{0,1},{1,2},{2,3},{3,4},{4,5},{5,6},{6,7},{7,8},{8,9},{9,10},{10,1... | collective-permute-start | bytes 196616 | tf_op jit(solution)/shard_map/ppermute | solution.py:16
  155.1 6.5 %collective-permute-done.17 = bf16[128,2,128]{0,2,1:T(8,128)(2,1)S(1)} collective-permute-done((bf16[128,2,128]{0,2,1:T(8,128)(2,1)S(1)}, bf16[128,2,128]{0,2,1:T(8,128)(2,1)S(1)}, u32[]{:S(2)}, u32[]{:S(2)}) %collective-permute-start.17) | collective-permute-done | bytes 65568 | tf_op jit(solution)/shard_map/ppermute | solution.py:16
  161.6 1.7 gather_fusion.10
  163.2 1.8 %fusion.28 = f32[8,128,128,1]{2,1,3,0:T(8,128)S(1)} fusion(bf16[1,8,4,128,128]{4,3,2,1,0:T(8,128)(2,1)S(1)} %copy-done, bf16[8,4,128,128]{2,3,1,0:T(8,128)(2,1)} %bitcast.308, pred[8,4]{1,0:T(8,128)(4,1)S(1)} %copy-done.22), kind=kOutput, calls=%fused_computation.56 | convolution fusion | flops 134742016 | bytes 2621472 | tf_op jit(solution)/shard_map/rkij,srkj->sri/dot_general | solution.py:61
  166.1 0.8 copy-done.12
  167.0 1.1 maximum_bitcast_fusion
  (113 shorter events, 15.6 us)
Async XLA Ops:
  0.0 21.3 %copy-start = (bf16[1,8,4,128,128]{4,3,2,1,0:T(8,128)(2,1)S(1)}, bf16[1,8,4,128,128]{4,3,2,1,0:T(8,128)(2,1)}, u32[]{:S(2)}) copy-start(bf16[1,8,4,128,128]{4,3,2,1,0:T(8,128)(2,1)} %param.15) | copy-start | bytes 3145732
  2.6 0.8 copy-start.14
  3.4 0.8 copy-start.8
  4.4 0.7 copy-start.15
  5.1 0.9 copy-start.1
  6.3 7.0 %copy-start.2 = (bf16[1,8,128,128]{3,2,1,0:T(8,128)(2,1)S(1)}, bf16[1,8,128,128]{3,2,1,0:T(8,128)(2,1)}, u32[]{:S(2)}) copy-start(bf16[1,8,128,128]{3,2,1,0:T(8,128)(2,1)} %param.14) | copy-start | bytes 786436
  6.4 7.3 %collective-permute-start.1 = (bf16[128,2,128]{0,2,1:T(8,128)(2,1)S(1)}, bf16[128,2,128]{0,2,1:T(8,128)(2,1)S(1)}, u32[]{:S(2)}, u32[]{:S(2)}) collective-permute-start(bf16[128,2,128]{0,2,1:T(8,128)(2,1)S(1)} %get-tuple-element.28), channel_id=1, source_target_pairs={{1,0},{2,1},{3,2},{4,3},{5,4},{6,5},{7,6},{8,7},{9,8},{10,9},{11,1... | collective-permute-start | bytes 196616 | tf_op jit(solution)/shard_map/ppermute | solution.py:17
  10.4 9.2 %collective-permute-start = (bf16[128,2,128]{0,2,1:T(8,128)(2,1)S(1)}, bf16[128,2,128]{0,2,1:T(8,128)(2,1)S(1)}, u32[]{:S(2)}, u32[]{:S(2)}) collective-permute-start(bf16[128,2,128]{0,2,1:T(8,128)(2,1)S(1)} %get-tuple-element.27), channel_id=1, source_target_pairs={{0,1},{1,2},{2,3},{3,4},{4,5},{5,6},{6,7},{7,8},{8,9},{9,10},{10,1... | collective-permute-start | bytes 196616 | tf_op jit(solution)/shard_map/ppermute | solution.py:16
  12.3 0.7 copy-start.16
  13.3 23.6 %copy-start.17 = (pred[8,4]{1,0:T(8,128)(4,1)}, pred[8,4]{1,0:T(8,128)(4,1)S(1)}, u32[]{:S(2)}) copy-start(pred[8,4]{1,0:T(8,128)(4,1)S(1)} %copy.42) | copy-start | bytes 100
  24.0 4.7 %collective-permute-start.3 = (bf16[128,2,128]{0,2,1:T(8,128)(2,1)S(1)}, bf16[128,2,128]{0,2,1:T(8,128)(2,1)S(1)}, u32[]{:S(2)}, u32[]{:S(2)}) collective-permute-start(bf16[128,2,128]{0,2,1:T(8,128)(2,1)S(1)} %get-tuple-element.26), channel_id=1, source_target_pairs={{1,0},{2,1},{3,2},{4,3},{5,4},{6,5},{7,6},{8,7},{9,8},{10,9},{11,1... | collective-permute-start | bytes 196616 | tf_op jit(solution)/shard_map/ppermute | solution.py:17
  25.9 9.3 %collective-permute-start.2 = (bf16[128,2,128]{0,2,1:T(8,128)(2,1)S(1)}, bf16[128,2,128]{0,2,1:T(8,128)(2,1)S(1)}, u32[]{:S(2)}, u32[]{:S(2)}) collective-permute-start(bf16[128,2,128]{0,2,1:T(8,128)(2,1)S(1)} %get-tuple-element.25), channel_id=1, source_target_pairs={{0,1},{1,2},{2,3},{3,4},{4,5},{5,6},{6,7},{7,8},{8,9},{9,10},{10,1... | collective-permute-start | bytes 196616 | tf_op jit(solution)/shard_map/ppermute | solution.py:16
  39.3 5.1 %copy-start.5 = (f32[16,8,8,128]{3,1,2,0:T(8,128)S(1)}, f32[16,8,8,128]{3,1,2,0:T(8,128)}, u32[]{:S(2)}) copy-start(f32[16,8,8,128]{3,1,2,0:T(8,128)} %get-tuple-element.10) | copy-start | bytes 1572868
  40.2 8.6 %collective-permute-start.4 = (bf16[128,256]{0,1:T(8,128)(2,1)S(1)}, bf16[128,256]{0,1:T(8,128)(2,1)S(1)}, u32[]{:S(2)}, u32[]{:S(2)}) collective-permute-start(bf16[128,256]{0,1:T(8,128)(2,1)S(1)} %bitcast.321), channel_id=1, source_target_pairs={{0,16},{16,32},{32,48},{48,64},{64,80},{80,96},{96,112},{112,128},... | collective-permute-start | bytes 196616 | tf_op jit(solution)/shard_map/ppermute | solution.py:25
  44.4 4.4 %copy-start.9 = (bf16[1,2,128,128]{3,2,1,0:T(8,128)(2,1)S(1)}, bf16[1,2,128,128]{3,2,1,0:T(8,128)(2,1)}, u32[]{:S(2)}) copy-start(bf16[1,2,128,128]{3,2,1,0:T(8,128)(2,1)} %param.18) | copy-start | bytes 196612
  49.7 4.7 %collective-permute-start.6 = (bf16[128,2,128]{0,2,1:T(8,128)(2,1)S(1)}, bf16[128,2,128]{0,2,1:T(8,128)(2,1)S(1)}, u32[]{:S(2)}, u32[]{:S(2)}) collective-permute-start(bf16[128,2,128]{0,2,1:T(8,128)(2,1)S(1)} %get-tuple-element.24), channel_id=1, source_target_pairs={{1,0},{2,1},{3,2},{4,3},{5,4},{6,5},{7,6},{8,7},{9,8},{10,9},{11,1... | collective-permute-start | bytes 196616 | tf_op jit(solution)/shard_map/ppermute | solution.py:17
  51.6 9.2 %collective-permute-start.5 = (bf16[128,2,128]{0,2,1:T(8,128)(2,1)S(1)}, bf16[128,2,128]{0,2,1:T(8,128)(2,1)S(1)}, u32[]{:S(2)}, u32[]{:S(2)}) collective-permute-start(bf16[128,2,128]{0,2,1:T(8,128)(2,1)S(1)} %get-tuple-element.23), channel_id=1, source_target_pairs={{0,1},{1,2},{2,3},{3,4},{4,5},{5,6},{6,7},{7,8},{8,9},{9,10},{10,1... | collective-permute-start | bytes 196616 | tf_op jit(solution)/shard_map/ppermute | solution.py:16
  62.6 0.7 copy-start.18
  65.9 4.7 %collective-permute-start.8 = (bf16[128,2,128]{0,2,1:T(8,128)(2,1)S(1)}, bf16[128,2,128]{0,2,1:T(8,128)(2,1)S(1)}, u32[]{:S(2)}, u32[]{:S(2)}) collective-permute-start(bf16[128,2,128]{0,2,1:T(8,128)(2,1)S(1)} %get-tuple-element.22), channel_id=1, source_target_pairs={{1,0},{2,1},{3,2},{4,3},{5,4},{6,5},{7,6},{8,7},{9,8},{10,9},{11,1... | collective-permute-start | bytes 196616 | tf_op jit(solution)/shard_map/ppermute | solution.py:17
  67.9 9.2 %collective-permute-start.7 = (bf16[128,2,128]{0,2,1:T(8,128)(2,1)S(1)}, bf16[128,2,128]{0,2,1:T(8,128)(2,1)S(1)}, u32[]{:S(2)}, u32[]{:S(2)}) collective-permute-start(bf16[128,2,128]{0,2,1:T(8,128)(2,1)S(1)} %get-tuple-element.21), channel_id=1, source_target_pairs={{0,1},{1,2},{2,3},{3,4},{4,5},{5,6},{6,7},{7,8},{8,9},{9,10},{10,1... | collective-permute-start | bytes 196616 | tf_op jit(solution)/shard_map/ppermute | solution.py:16
  78.8 0.7 copy-start.19
  81.8 2.9 %copy-start.4 = (f32[16,8,8,128]{3,1,2,0:T(8,128)S(1)}, f32[16,8,8,128]{3,1,2,0:T(8,128)}, u32[]{:S(2)}) copy-start(f32[16,8,8,128]{3,1,2,0:T(8,128)} %get-tuple-element.12) | copy-start | bytes 1572868
  82.2 2.6 %copy-start.6 = (bf16[128,8,128]{0,2,1:T(8,128)(2,1)}, bf16[128,8,128]{0,2,1:T(8,128)(2,1)S(1)}, u32[]{:S(2)}) copy-start(bf16[128,8,128]{0,2,1:T(8,128)(2,1)S(1)} %fusion.20) | copy-start | bytes 786436
  82.8 8.3 %collective-permute-start.9 = (bf16[128,256]{0,1:T(8,128)(2,1)S(1)}, bf16[128,256]{0,1:T(8,128)(2,1)S(1)}, u32[]{:S(2)}, u32[]{:S(2)}) collective-permute-start(bf16[128,256]{0,1:T(8,128)(2,1)S(1)} %bitcast.322), channel_id=1, source_target_pairs={{0,16},{16,32},{32,48},{48,64},{64,80},{80,96},{96,112},{112,128},... | collective-permute-start | bytes 196616 | tf_op jit(solution)/shard_map/ppermute | solution.py:25
  84.8 6.3 %copy-start.10 = (bf16[1,2,128,128]{3,2,1,0:T(8,128)(2,1)S(1)}, bf16[1,2,128,128]{3,2,1,0:T(8,128)(2,1)}, u32[]{:S(2)}) copy-start(bf16[1,2,128,128]{3,2,1,0:T(8,128)(2,1)} %param.18) | copy-start | bytes 196612
  92.0 4.7 %collective-permute-start.11 = (bf16[128,2,128]{0,2,1:T(8,128)(2,1)S(1)}, bf16[128,2,128]{0,2,1:T(8,128)(2,1)S(1)}, u32[]{:S(2)}, u32[]{:S(2)}) collective-permute-start(bf16[128,2,128]{0,2,1:T(8,128)(2,1)S(1)} %get-tuple-element.20), channel_id=1, source_target_pairs={{1,0},{2,1},{3,2},{4,3},{5,4},{6,5},{7,6},{8,7},{9,8},{10,9},{11,1... | collective-permute-start | bytes 196616 | tf_op jit(solution)/shard_map/ppermute | solution.py:17
  93.9 9.2 %collective-permute-start.10 = (bf16[128,2,128]{0,2,1:T(8,128)(2,1)S(1)}, bf16[128,2,128]{0,2,1:T(8,128)(2,1)S(1)}, u32[]{:S(2)}, u32[]{:S(2)}) collective-permute-start(bf16[128,2,128]{0,2,1:T(8,128)(2,1)S(1)} %get-tuple-element.19), channel_id=1, source_target_pairs={{0,1},{1,2},{2,3},{3,4},{4,5},{5,6},{6,7},{7,8},{8,9},{9,10},{10,1... | collective-permute-start | bytes 196616 | tf_op jit(solution)/shard_map/ppermute | solution.py:16
  104.8 0.7 copy-start.20
  108.2 4.9 %collective-permute-start.13 = (bf16[128,2,128]{0,2,1:T(8,128)(2,1)S(1)}, bf16[128,2,128]{0,2,1:T(8,128)(2,1)S(1)}, u32[]{:S(2)}, u32[]{:S(2)}) collective-permute-start(bf16[128,2,128]{0,2,1:T(8,128)(2,1)S(1)} %get-tuple-element.18), channel_id=1, source_target_pairs={{1,0},{2,1},{3,2},{4,3},{5,4},{6,5},{7,6},{8,7},{9,8},{10,9},{11,1... | collective-permute-start | bytes 196616 | tf_op jit(solution)/shard_map/ppermute | solution.py:17
  110.1 9.2 %collective-permute-start.12 = (bf16[128,2,128]{0,2,1:T(8,128)(2,1)S(1)}, bf16[128,2,128]{0,2,1:T(8,128)(2,1)S(1)}, u32[]{:S(2)}, u32[]{:S(2)}) collective-permute-start(bf16[128,2,128]{0,2,1:T(8,128)(2,1)S(1)} %get-tuple-element.17), channel_id=1, source_target_pairs={{0,1},{1,2},{2,3},{3,4},{4,5},{5,6},{6,7},{7,8},{8,9},{9,10},{10,1... | collective-permute-start | bytes 196616 | tf_op jit(solution)/shard_map/ppermute | solution.py:16
  121.0 0.7 copy-start.21
  124.1 2.9 %copy-start.3 = (f32[16,8,8,128]{3,1,2,0:T(8,128)S(1)}, f32[16,8,8,128]{3,1,2,0:T(8,128)}, u32[]{:S(2)}) copy-start(f32[16,8,8,128]{3,1,2,0:T(8,128)} %get-tuple-element.11) | copy-start | bytes 1572868
  125.0 8.3 %collective-permute-start.14 = (bf16[128,256]{0,1:T(8,128)(2,1)S(1)}, bf16[128,256]{0,1:T(8,128)(2,1)S(1)}, u32[]{:S(2)}, u32[]{:S(2)}) collective-permute-start(bf16[128,256]{0,1:T(8,128)(2,1)S(1)} %bitcast.320), channel_id=1, source_target_pairs={{0,16},{16,32},{32,48},{48,64},{64,80},{80,96},{96,112},{112,128},... | collective-permute-start | bytes 196616 | tf_op jit(solution)/shard_map/ppermute | solution.py:25
  127.1 1.0 copy-start.7
  128.9 4.4 %copy-start.11 = (bf16[1,2,128,128]{3,2,1,0:T(8,128)(2,1)S(1)}, bf16[1,2,128,128]{3,2,1,0:T(8,128)(2,1)}, u32[]{:S(2)}) copy-start(bf16[1,2,128,128]{3,2,1,0:T(8,128)(2,1)} %param.18) | copy-start | bytes 196612
  134.2 4.7 %collective-permute-start.16 = (bf16[128,2,128]{0,2,1:T(8,128)(2,1)S(1)}, bf16[128,2,128]{0,2,1:T(8,128)(2,1)S(1)}, u32[]{:S(2)}, u32[]{:S(2)}) collective-permute-start(bf16[128,2,128]{0,2,1:T(8,128)(2,1)S(1)} %get-tuple-element.16), channel_id=1, source_target_pairs={{1,0},{2,1},{3,2},{4,3},{5,4},{6,5},{7,6},{8,7},{9,8},{10,9},{11,1... | collective-permute-start | bytes 196616 | tf_op jit(solution)/shard_map/ppermute | solution.py:17
  136.1 9.2 %collective-permute-start.15 = (bf16[128,2,128]{0,2,1:T(8,128)(2,1)S(1)}, bf16[128,2,128]{0,2,1:T(8,128)(2,1)S(1)}, u32[]{:S(2)}, u32[]{:S(2)}) collective-permute-start(bf16[128,2,128]{0,2,1:T(8,128)(2,1)S(1)} %get-tuple-element.15), channel_id=1, source_target_pairs={{0,1},{1,2},{2,3},{3,4},{4,5},{5,6},{6,7},{7,8},{8,9},{9,10},{10,1... | collective-permute-start | bytes 196616 | tf_op jit(solution)/shard_map/ppermute | solution.py:16
  147.0 0.7 copy-start.22
  150.4 4.7 %collective-permute-start.18 = (bf16[128,2,128]{0,2,1:T(8,128)(2,1)S(1)}, bf16[128,2,128]{0,2,1:T(8,128)(2,1)S(1)}, u32[]{:S(2)}, u32[]{:S(2)}) collective-permute-start(bf16[128,2,128]{0,2,1:T(8,128)(2,1)S(1)} %get-tuple-element.14), channel_id=1, source_target_pairs={{1,0},{2,1},{3,2},{4,3},{5,4},{6,5},{7,6},{8,7},{9,8},{10,9},{11,1... | collective-permute-start | bytes 196616 | tf_op jit(solution)/shard_map/ppermute | solution.py:17
  152.3 9.2 %collective-permute-start.17 = (bf16[128,2,128]{0,2,1:T(8,128)(2,1)S(1)}, bf16[128,2,128]{0,2,1:T(8,128)(2,1)S(1)}, u32[]{:S(2)}, u32[]{:S(2)}) collective-permute-start(bf16[128,2,128]{0,2,1:T(8,128)(2,1)S(1)} %get-tuple-element.13), channel_id=1, source_target_pairs={{0,1},{1,2},{2,3},{3,4},{4,5},{5,6},{6,7},{7,8},{8,9},{9,10},{10,1... | collective-permute-start | bytes 196616 | tf_op jit(solution)/shard_map/ppermute | solution.py:16
  165.9 1.0 copy-start.12
  166.0 1.0 copy-start.13
where the time goes:
time: 169 us; the launch traced here: 168 us
  waiting for transfers between devices  65.1 us (39%)
  starting transfers between devices  44.3 us (26%)
  local copies, waits for them, and re-layouts  26.2 us (16%)
  matrix products  22.7 us (13%)
  other arithmetic  9.08 us (5%)
    ppermute x8, waiting for transfers between devices, padded(): before = lax.ppermute(last, axis, up)  50.9 us
    ppermute x8, starting transfers between devices, padded(): before = lax.ppermute(last, axis, up)  18.9 us
    ppermute x8, starting transfers between devices, padded(): after = lax.ppermute(leading, axis, down)  17.5 us
    dot_general x8, matrix products, on_device(): jnp.einsum('rkij,srkj->sri', neighbours, gathered, preferred_element_type...  14.2 us
    ppermute x3, waiting for transfers between devices, from_behind(): return lax.ppermute(block, axis, route)  14.1 us
    gather x8, local copies, waits for them, and re-layouts, on_device(): gathered = jnp.take(extended, local_cols, axis=1)  13.2 us
    unnamed x50, local copies, waits for them, and re-layouts  8.95 us
    ppermute x3, starting transfers between devices, from_behind(): return lax.ppermute(block, axis, route)  7.93 us
  transfers between devices with their start and end apart: 19, of which 11 were waited for; matrix products, arithmetic and copies ran while one was open for 3% of the time, Pallas kernels for 0%

commit v1 on v0

v1 whole, which is shorter than its diff:
```python
import functools

import jax
import jax.numpy as jnp
from jax import lax
from jax.experimental import pallas as pl
from jax.experimental.pallas import tpu as pltpu
from jax.sharding import PartitionSpec as P

HALO = 2
MESH = pl.DeviceIdType.MESH
BF16 = jnp.bfloat16
F32 = jnp.float32


def mm(u, w):
    return lax.dot_general(u, w, (((1,), (1,)), ((), ())), preferred_element_type=F32)


def kernel(S, FN, T, N, K, Q, W, *refs):
    refs = list(refs)
    take = lambda n: [refs.pop(0) for _ in range(n)]
    cols, iface, rhs, inflow, diag, off, inv, coup = take(8)
    (out,) = take(1)
    rhs_v, diag_v, off_v, inv_v, coup_v, out_v, sent = take(7)
    incs = take(T)
    rights = take(T)
    fields = take(2 * T)
    ld, st, hs, hr, ssem, rsem = take(6)

    s = lax.axis_index("slab")
    f = lax.axis_index("face")
    has_l, has_r = f > 0, f < FN - 1
    has_p, has_n = s > 0, s < S - 1
    left = (s, jnp.maximum(f - 1, 0))
    right = (s, jnp.minimum(f + 1, FN - 1))
    prev = (jnp.maximum(s - 1, 0), f)
    nxt = (jnp.minimum(s + 1, S - 1), f)

    barrier = pltpu.get_barrier_semaphore()
    for there, who in ((has_l, left), (has_r, right), (has_p, prev), (has_n, nxt)):
        @pl.when(there)
        def _(who=who):
            pl.semaphore_signal(barrier, inc=1, device_id=who, device_id_type=MESH)

    loads = [pltpu.make_async_copy(inflow.at[0, :, q * W:(q + 1) * W], incs[0].at[q], ld.at[q]) for q in range(Q)]
    loads += [
        pltpu.make_async_copy(coup.at[0], coup_v, ld.at[Q]),
        pltpu.make_async_copy(rhs.at[0, 0], rhs_v.at[0], ld.at[Q + 1]),
        pltpu.make_async_copy(inv.at[0], inv_v, ld.at[Q + 2]),
        pltpu.make_async_copy(diag.at[0], diag_v, ld.at[Q + 3]),
        pltpu.make_async_copy(off.at[0], off_v, ld.at[Q + 4]),
    ]
    loads += [pltpu.make_async_copy(rhs.at[t, 0], rhs_v.at[t], ld.at[Q + 4 + t]) for t in range(1, T)]
    for c in loads:
        c.start()

    base = f * N - HALO

    def col(r, k):
        return jnp.clip(cols[k, r] - base, 0, N + 2 * HALO - 1)

    local = [[col(r, k) for k in range(K)] for r in range(N)]
    e = [iface[q] for q in range(Q)]

    zero_halo = jnp.zeros((HALO,) + fields[0].shape[1:], BF16)
    for b in fields:
        @pl.when(f == 0)
        def _(b=b):
            b[0:HALO] = zero_halo

        @pl.when(f == FN - 1)
        def _(b=b):
            b[N + HALO:N + 2 * HALO] = zero_halo

    for t in range(1, T):
        @pl.when(s == 0)
        def _(t=t):
            incs[t][...] = jnp.zeros(incs[t].shape, BF16)

    def halo(i, side):
        b = fields[i]
        if side == 0:
            src, dst, dev = b.at[HALO:2 * HALO], b.at[N + HALO:N + 2 * HALO], left
        else:
            src, dst, dev = b.at[N:N + HALO], b.at[0:HALO], right
        return pltpu.make_async_remote_copy(src_ref=src, dst_ref=dst, send_sem=hs.at[i, side], recv_sem=hr.at[i, side], device_id=dev, device_id_type=MESH)

    def send_halo(i, side):
        @pl.when(has_l if side == 0 else has_r)
        def _():
            halo(i, side).start()

    def wait_halo(i):
        @pl.when(has_r)
        def _():
            halo(i, 0).wait_recv()

        @pl.when(has_l)
        def _():
            halo(i, 1).wait_recv()

    def forward(t):
        return pltpu.make_async_remote_copy(src_ref=sent.at[t], dst_ref=incs[t + 1], send_sem=ssem.at[t], recv_sem=rsem.at[t], device_id=nxt, device_id_type=MESH)

    def step(b, right_b, r, cs):
        u = jnp.concatenate([b[r + HALO]] + [b[c] for c in cs], axis=1)
        w = jnp.concatenate([diag_v[r]] + [off_v[r, k] for k in range(K)], axis=1)
        corr = (right_b[r].astype(F32) - mm(u, w)).astype(BF16)
        return (b[r + HALO].astype(F32) + mm(corr, inv_v[r])).astype(BF16)

    order = [0, 1, N - 2, N - 1] + list(range(2, N - 2))
    stores = []
    for t in range(T):
        inc, rb, fa, fb = incs[t], rights[t], fields[2 * t], fields[2 * t + 1]
        if t == 0:
            for c in loads[:Q + 3]:
                c.wait()
        else:
            loads[Q + 4 + t].wait()

            @pl.when(has_p)
            def _(t=t):
                forward(t - 1).wait_recv()
        coupled = [mm(inc[q], coup_v[q]) for q in range(Q)]
        for n, r in enumerate(order):
            x = rhs_v[t, :, r * W:(r + 1) * W].astype(F32)
            for q in range(Q):
                x = x - jnp.where(e[q] == r, coupled[q], 0.0)
            x = x.astype(BF16)
            rb[r] = x
            fa[r + HALO] = mm(x, inv_v[r]).astype(BF16)
            if n == 3:
                if t == 0:
                    pl.semaphore_wait(barrier, has_l.astype(jnp.int32) + has_r.astype(jnp.int32) + has_p.astype(jnp.int32) + has_n.astype(jnp.int32))
                send_halo(2 * t, 0)
                send_halo(2 * t, 1)
        if t == 0:
            loads[Q + 3].wait()
            loads[Q + 4].wait()
        wait_halo(2 * t)
        for n, r in enumerate(order):
            fb[r + HALO] = step(fa, rb, r, local[r])
            if n == 3:
                send_halo(2 * t + 1, 0)
                send_halo(2 * t + 1, 1)
        wait_halo(2 * t + 1)
        if t + 1 < T:
            for q in range(Q):
                sent[t, q] = step(fb, rb, e[q], [col(e[q], k) for k in range(K)])

            @pl.when(has_n)
            def _(t=t):
                forward(t).start()
        for r in range(N):
            out_v[t, :, r * W:(r + 1) * W] = step(fb, rb, r, local[r])
        c = pltpu.make_async_copy(out_v.at[t], out.at[t, 0], st.at[t])
        c.start()
        stores.append(c)

    for i in range(2 * T):
        @pl.when(has_l)
        def _(i=i):
            halo(i, 0).wait_send()

        @pl.when(has_r)
        def _(i=i):
            halo(i, 1).wait_send()
    for t in range(T - 1):
        @pl.when(has_n)
        def _(t=t):
            forward(t).wait_send()
    for c in stores:
        c.wait()


def on_device(S, FN, rhs, inflow, diag, off, cols, inv, coup, iface):
    T, _, M, _ = rhs.shape
    _, N, K, W, _ = off.shape
    Q = coup.shape[1]
    ANY = pl.BlockSpec(memory_space=pl.ANY)
    SM = pl.BlockSpec(memory_space=pltpu.SMEM)
    DMA = pltpu.SemaphoreType.DMA
    return pl.pallas_call(
        functools.partial(kernel, S, FN, T, N, K, Q, W),
        out_shape=jax.ShapeDtypeStruct(rhs.shape, BF16),
        in_specs=[SM, SM] + [ANY] * 6,
        out_specs=ANY,
        scratch_shapes=[
            pltpu.VMEM((T, M, N * W), BF16),
            pltpu.VMEM((N, W, W), BF16),
            pltpu.VMEM((N, K, W, W), BF16),
            pltpu.VMEM((N, W, W), BF16),
            pltpu.VMEM((Q, W, W), BF16),
            pltpu.VMEM((T, M, N * W), BF16),
            pltpu.VMEM((T - 1, Q, M, W), BF16),
        ]
        + [pltpu.VMEM((Q, M, W), BF16)] * T
        + [pltpu.VMEM((N, M, W), BF16)] * T
        + [pltpu.VMEM((N + 2 * HALO, M, W), BF16)] * (2 * T)
        + [DMA((Q + 4 + T,)), DMA((T,)), DMA((2 * T, 2)), DMA((2 * T, 2)), DMA((T - 1,)), DMA((T - 1,))],
        compiler_params=pltpu.CompilerParams(collective_id=0, has_side_effects=True, vmem_limit_bytes=64000000),
        name="sweep",
    )(cols[0].T, iface, rhs, inflow, diag, off, inv, coup)


def solution(mesh):
    placed = (
        P(None, "slab", None, "face"),
        P("slab", None, "face"),
        P("slab", "face", None, None),
        P("slab", "face", None, None, None),
        P("slab", "face", None),
        P("slab", "face", None, None),
        P("slab", "face", None, None),
        P("face"),
    )
    return jax.shard_map(
        functools.partial(on_device, mesh.shape["slab"], mesh.shape["face"]),
        mesh=mesh,
        in_specs=placed,
        out_specs=P(None, "slab", None, "face"),
        check_vma=False,
    )
```

time: 169 us -> 64.2 us (0.38)
  waiting for transfers between devices: 65.1 us -> 0 us
  Pallas kernels: 0 us -> 61.8 us
  starting transfers between devices: 44.3 us -> 0 us
  local copies, waits for them, and re-layouts: 26.2 us -> 2.26 us
  matrix products: 22.7 us -> 0 us
  other arithmetic: 9.08 us -> 0 us
    ppermute x19 -> x0, waiting for transfers between devices: 65.1 us -> none  [the longest x8 50.9 us: padded(): before = lax.ppermute(last, axis, up)]
    pallas_call x0 -> x1, Pallas kernels: none -> 61.8 us  [on_device(): pl.pallas_call(functools.partial(kernel, S, FN, T, N, K, Q, W), out_shape...]
    ppermute x19 -> x0, starting transfers between devices: 44.3 us -> none  [the longest x8 18.9 us: padded(): before = lax.ppermute(last, axis, up)]
    dot_general x36 -> x0, matrix products: 22.7 us -> none  [the longest x8 14.2 us: on_device(): jnp.einsum('rkij,srkj->sri', neighbours, gathered, preferred_element_type...]
    gather x11 -> x0, local copies, waits for them, and re-layouts: 14.9 us -> none  [the longest x8 13.2 us: on_device(): gathered = jnp.take(extended, local_cols, axis=1)]
    unnamed x50 -> x1, local copies, waits for them, and re-layouts: 8.95 us -> 2.26 us
    convert_element_type x8 -> x0, other arithmetic: 4.76 us -> none  [on_device(): correction = (right.astype(jnp.float32) - product).astype(jnp.bfloat16)]
    unnamed x1 -> x0, other arithmetic: 2.55 us -> none
  transfers between devices with their start and end apart: 19 -> 0, of which waited for: 11 -> 0; matrix products, arithmetic and copies ran while one was open for 3% -> 0% of each run, Pallas kernels for 0% -> 0%
where the time goes in v1:
time: 64.2 us; the launch traced here: 64.1 us
  Pallas kernels  61.8 us (96%)
  local copies, waits for them, and re-layouts  2.26 us (4%)
    pallas_call x1, Pallas kernels, on_device(): pl.pallas_call(functools.partial(kernel, S, FN, T, N, K, Q, W), out_shape...  61.8 us
    unnamed x1, local copies, waits for them, and re-layouts  2.26 us

profile of v1, /device:TPU:400, one launch (start us, length us, event | category | flops | bytes accessed | tf_op | source)
XLA Modules:
  0.0 64.1 jit_solution(14712884557835755650)
XLA Ops:
  0.0 61.8 %sweep.1 = bf16[4,1,128,1024]{3,2,1,0:T(8,128)(2,1)} custom-call(s32[4,8]{1,0:T(4,128)} %bitcast.3, s32[2]{0:T(128)} %refs_1_.1, bf16[4,1,128,1024]{3,2,1,0:T(8,128)(2,1)} %refs_2_.1, bf16[1,128,256]{2,1,0:T(8,128)(2,1)} %refs_3_.1, bf16[1,8,128,128]{3,2,1,0:T(8,128)(2,1)} %refs_4_.1, bf16[1,8,4,128,128]{4,3,2,1,0:T(8,128)(2,1)} %refs_5_.1, ...), custom_call_target="tpu_custom_call" | custom-call | tf_op jit(solution)/shard_map/sweep/pallas_call | solution.py:184
  61.8 2.3 %copy.10 = bf16[4,1,128,1024]{3,2,1,0:T(8,128)(2,1)} copy(bf16[4,1,128,1024]{3,2,1,0:T(8,128)(2,1)} %sweep.1) | data formatting | bytes 2097152

commit v2 on v1

v2 whole, which is shorter than its diff:
```python
import functools

import jax
import jax.numpy as jnp
from jax import lax
from jax.experimental import pallas as pl
from jax.experimental.pallas import tpu as pltpu
from jax.sharding import PartitionSpec as P

HALO = 2
MESH = pl.DeviceIdType.MESH
BF16 = jnp.bfloat16
F32 = jnp.float32


def mm(u, w):
    return lax.dot_general(u, w, (((1,), (1,)), ((), ())), preferred_element_type=F32)


def kernel(S, FN, T, N, K, Q, W, *refs):
    refs = list(refs)
    take = lambda n: [refs.pop(0) for _ in range(n)]
    cols, iface, rhs, inflow, diag, off, inv, coup = take(8)
    (out,) = take(1)
    rhs_v, diag_v, off_v, inv_v, coup_v, out_v, sent = take(7)
    z, part, ypart, h1send, y_in = take(5)
    incs = take(T)
    rights = take(T)
    f0, f1 = take(T), take(T)
    n0, o0, n1, o1 = take(T), take(T), take(T), take(T)
    ld, st, hs, hr, ysem, ssem, rsem = take(7)

    s = lax.axis_index("slab")
    f = lax.axis_index("face")
    odd = lax.rem(f, 2)
    has_o = (f > 0) & (f < FN - 1)
    has_p, has_n = s > 0, s < S - 1
    near = (s, f + 1 - 2 * odd)
    other = (s, jnp.clip(f - 1 + 2 * odd, 0, FN - 1))
    prev = (jnp.maximum(s - 1, 0), f)
    nxt = (jnp.minimum(s + 1, S - 1), f)
    oe = odd * (N - HALO)
    ne = (N - HALO) - oe
    o_slot = odd * (N + HALO)
    n_slot = (N + HALO) - o_slot

    barrier = pltpu.get_barrier_semaphore()
    pl.semaphore_signal(barrier, inc=1, device_id=near, device_id_type=MESH)
    for there, who in ((has_o, other), (has_p, prev), (has_n, nxt)):
        @pl.when(there)
        def _(who=who):
            pl.semaphore_signal(barrier, inc=1, device_id=who, device_id_type=MESH)

    loads = [pltpu.make_async_copy(inflow.at[0, :, q * W:(q + 1) * W], incs[0].at[q], ld.at[q]) for q in range(Q)]
    loads += [
        pltpu.make_async_copy(coup.at[0], coup_v, ld.at[Q]),
        pltpu.make_async_copy(rhs.at[0, 0], rhs_v.at[0], ld.at[Q + 1]),
        pltpu.make_async_copy(inv.at[0], inv_v, ld.at[Q + 2]),
        pltpu.make_async_copy(off.at[0], off_v, ld.at[Q + 4]),
        pltpu.make_async_copy(diag.at[0], diag_v, ld.at[Q + 3]),
    ]
    loads += [pltpu.make_async_copy(rhs.at[t, 0], rhs_v.at[t], ld.at[Q + 4 + t]) for t in range(1, T)]
    for c in loads:
        c.start()

    base = f * N - HALO

    def col(r, k):
        return jnp.clip(cols[k, r] - base, 0, N + 2 * HALO - 1)

    e = [iface[q] for q in range(Q)]

    zero_halo = jnp.zeros((HALO,) + f0[0].shape[1:], BF16)
    for b in f0 + f1:
        b[0:HALO] = zero_halo
        b[N + HALO:N + 2 * HALO] = zero_halo

    @pl.when(jnp.logical_not(has_o))
    def _():
        for b in o0 + o1:
            b[...] = zero_halo
        y_in[...] = jnp.zeros(y_in.shape, BF16)

    @pl.when(s == 0)
    def _():
        for b in incs[1:]:
            b[...] = jnp.zeros(b.shape, BF16)

    def to_near(i, src, dst):
        return pltpu.make_async_remote_copy(src_ref=src, dst_ref=dst, send_sem=hs.at[i, 0], recv_sem=hr.at[i, 0], device_id=near, device_id_type=MESH)

    def to_other(i, src, dst):
        return pltpu.make_async_remote_copy(src_ref=src, dst_ref=dst, send_sem=hs.at[i, 1], recv_sem=hr.at[i, 1], device_id=other, device_id_type=MESH)

    def copies(t):
        edge = lambda b, r: b.at[pl.ds(r + HALO, HALO)]
        return (
            to_near(2 * t, edge(f0[t], ne), n0[t]),
            to_other(2 * t, edge(f0[t], oe), o0[t]),
            to_near(2 * t + 1, edge(f1[t], ne), n1[t]),
            to_other(2 * t + 1, h1send.at[t], o1[t]),
        )

    def y_copy():
        return pltpu.make_async_remote_copy(src_ref=z.at[pl.ds(oe, HALO), :, HALO * W:2 * HALO * W], dst_ref=y_in, send_sem=ysem.at[0], recv_sem=ysem.at[1], device_id=other, device_id_type=MESH)

    def forward(t):
        return pltpu.make_async_remote_copy(src_ref=sent.at[t], dst_ref=incs[t + 1], send_sem=ssem.at[t], recv_sem=rsem.at[t], device_id=nxt, device_id_type=MESH)

    def when_o(act):
        @pl.when(has_o)
        def _():
            act()

    def own(b, right_b, r):
        u = jnp.concatenate([b[r + HALO]] + [b[col(r, k)] for k in range(K)], axis=1)
        w = jnp.concatenate([diag_v[r]] + [off_v[r, k] for k in range(K)], axis=1)
        corr = (right_b[r].astype(F32) - mm(u, w)).astype(BF16)
        return b[r + HALO].astype(F32) + mm(corr, inv_v[r])

    def halo_operator(r):
        tiles = [off_v[r, k].astype(F32) for k in range(K)]
        cs = [col(r, k) for k in range(K)]
        sums = []
        for slot in [n_slot + j for j in range(HALO)] + [o_slot + j for j in range(HALO)]:
            x = jnp.zeros((W, W), F32)
            for k in range(K):
                x = x + jnp.where(cs[k] == slot, tiles[k], 0.0)
            sums.append(x.astype(BF16))
        z[r] = jnp.dot(inv_v[r], jnp.concatenate(sums, axis=1), preferred_element_type=F32).astype(BF16)

    def pair(b):
        return jnp.concatenate([b[0], b[1]], axis=1)

    ZN, ZO = slice(0, HALO * W), slice(HALO * W, 2 * HALO * W)
    order = [oe, oe + 1, ne, ne + 1] + list(range(HALO, N - HALO))
    stores = []
    for t in range(T):
        inc, rb, fa, fb = incs[t], rights[t], f0[t], f1[t]
        near0, other0, near1, other1 = copies(t)
        if t == 0:
            for c in loads[:Q + 3]:
                c.wait()
        else:
            loads[Q + 4 + t].wait()

            @pl.when(has_p)
            def _(t=t):
                forward(t - 1).wait_recv()
        coupled = [mm(inc[q], coup_v[q]) for q in range(Q)]
        for n, r in enumerate(order):
            x = rhs_v[t, :, pl.ds(pl.multiple_of(r * W, W), W)].astype(F32)
            for q in range(Q):
                x = x - jnp.where(e[q] == r, coupled[q], 0.0)
            x = x.astype(BF16)
            rb[r] = x
            fa[r + HALO] = mm(x, inv_v[r]).astype(BF16)
            if n == 3:
                if t == 0:
                    pl.semaphore_wait(barrier, 1 + has_o.astype(jnp.int32) + has_p.astype(jnp.int32) + has_n.astype(jnp.int32))
                when_o(other0.start)
                near0.start()
        if t == 0:
            loads[Q + 3].wait()
            for r in order[:2]:
                halo_operator(r)
            when_o(lambda: y_copy().start())
            loads[Q + 4].wait()
        for r in order[:2]:
            part[r] = own(fa, rb, r)
        near0.wait_recv()
        hn = pair(n0[t])
        for i, r in enumerate(order[:2]):
            x = part[r] - mm(hn, z[r, :, ZN])
            part[r] = x
            h1send[t, i] = x.astype(BF16)
        when_o(other1.start)
        for r in order[2:]:
            if t == 0:
                halo_operator(r)
            part[r] = own(fa, rb, r) - mm(hn, z[r, :, ZN])
        if t == 0:
            when_o(lambda: y_copy().wait_recv())
        mine = jnp.concatenate([fa[oe + HALO], fa[oe + HALO + 1]], axis=1)
        for i in range(HALO):
            ypart[i] = mm(mine, y_in[i])
        when_o(other0.wait_recv)
        ho = pair(o0[t])
        for n, r in enumerate(order[2:4] + order[:2] + order[4:]):
            fb[r + HALO] = (part[r] - mm(ho, z[r, :, ZO])).astype(BF16)
            if n == 1:
                near1.start()
        if t + 1 < T:
            mid = [own(fb, rb, e[q]) for q in range(Q)]
        else:
            mid = []
            for r in range(N):
                part[r] = own(fb, rb, r)
        near1.wait_recv()
        when_o(other1.wait_recv)
        far = [(o1[t][i].astype(F32) - ypart[i]).astype(BF16) for i in range(HALO)]
        both = jnp.concatenate([n1[t][0], n1[t][1]] + far, axis=1)
        if t + 1 < T:
            for q in range(Q):
                sent[t, q] = (mid[q] - mm(both, z[e[q]])).astype(BF16)

            @pl.when(has_n)
            def _(t=t):
                forward(t).start()
            for r in range(N):
                part[r] = own(fb, rb, r)
        for r in range(N):
            out_v[t, :, r * W:(r + 1) * W] = (part[r] - mm(both, z[r])).astype(BF16)
        c = pltpu.make_async_copy(out_v.at[t], out.at[t, 0], st.at[t])
        c.start()
        stores.append(c)

    for t in range(T):
        near0, other0, near1, other1 = copies(t)
        near0.wait_send()
        near1.wait_send()
        when_o(other0.wait_send)
        when_o(other1.wait_send)
    when_o(lambda: y_copy().wait_send())
    for t in range(T - 1):
        @pl.when(has_n)
        def _(t=t):
            forward(t).wait_send()
    for c in stores:
        c.wait()


def on_device(S, FN, rhs, inflow, diag, off, cols, inv, coup, iface):
    T, _, M, _ = rhs.shape
    _, N, K, W, _ = off.shape
    Q = coup.shape[1]
    ANY = pl.BlockSpec(memory_space=pl.ANY)
    SM = pl.BlockSpec(memory_space=pltpu.SMEM)
    DMA = pltpu.SemaphoreType.DMA
    return pl.pallas_call(
        functools.partial(kernel, S, FN, T, N, K, Q, W),
        out_shape=jax.ShapeDtypeStruct(rhs.shape, BF16),
        in_specs=[SM, SM] + [ANY] * 6,
        out_specs=ANY,
        scratch_shapes=[
            pltpu.VMEM((T, M, N * W), BF16),
            pltpu.VMEM((N, W, W), BF16),
            pltpu.VMEM((N, K, W, W), BF16),
            pltpu.VMEM((N, W, W), BF16),
            pltpu.VMEM((Q, W, W), BF16),
            pltpu.VMEM((T, M, N * W), BF16),
            pltpu.VMEM((T - 1, Q, M, W), BF16),
        ]
        + [
            pltpu.VMEM((N, W, 2 * HALO * W), BF16),
            pltpu.VMEM((N, M, W), F32),
            pltpu.VMEM((HALO, M, W), F32),
            pltpu.VMEM((T, HALO, M, W), BF16),
            pltpu.VMEM((HALO, W, HALO * W), BF16),
        ]
        + [pltpu.VMEM((Q, M, W), BF16)] * T
        + [pltpu.VMEM((N, M, W), BF16)] * T
        + [pltpu.VMEM((N + 2 * HALO, M, W), BF16)] * (2 * T)
        + [pltpu.VMEM((HALO, M, W), BF16)] * (4 * T)
        + [DMA((Q + 4 + T,)), DMA((T,)), DMA((2 * T, 2)), DMA((2 * T, 2)), DMA((2,)), DMA((T - 1,)), DMA((T - 1,))],
        compiler_params=pltpu.CompilerParams(collective_id=0, has_side_effects=True, vmem_limit_bytes=64000000),
        name="sweep",
    )(cols[0].T, iface, rhs, inflow, diag, off, inv, coup)


def solution(mesh):
    placed = (
        P(None, "slab", None, "face"),
        P("slab", None, "face"),
        P("slab", "face", None, None),
        P("slab", "face", None, None, None),
        P("slab", "face", None),
        P("slab", "face", None, None),
        P("slab", "face", None, None),
        P("face"),
    )
    return jax.shard_map(
        functools.partial(on_device, mesh.shape["slab"], mesh.shape["face"]),
        mesh=mesh,
        in_specs=placed,
        out_specs=P(None, "slab", None, "face"),
        check_vma=False,
    )
```

time: 64.2 us -> 49.3 us (0.77)
  the two profiles are of different devices: /device:TPU:400 before, /device:TPU:391 now
where the time goes in v2:
time: 49.3 us; the launch traced here: 49.1 us
  Pallas kernels  46.8 us (95%)
  local copies, waits for them, and re-layouts  2.26 us (5%)
    pallas_call x1, Pallas kernels, on_device(): pl.pallas_call(functools.partial(kernel, S, FN, T, N, K, Q, W), out_shape...  46.8 us
    unnamed x1, local copies, waits for them, and re-layouts  2.26 us

profile of v2, /device:TPU:391, one launch (start us, length us, event | category | flops | bytes accessed | tf_op | source)
XLA Modules:
  0.0 49.1 jit_solution(2289780417897094644)
XLA Ops:
  0.0 46.8 %sweep.1 = bf16[4,1,128,1024]{3,2,1,0:T(8,128)(2,1)} custom-call(s32[4,8]{1,0:T(4,128)} %bitcast.3, s32[2]{0:T(128)} %refs_1_.1, bf16[4,1,128,1024]{3,2,1,0:T(8,128)(2,1)} %refs_2_.1, bf16[1,128,256]{2,1,0:T(8,128)(2,1)} %refs_3_.1, bf16[1,8,128,128]{3,2,1,0:T(8,128)(2,1)} %refs_4_.1, bf16[1,8,4,128,128]{4,3,2,1,0:T(8,128)(2,1)} %refs_5_.1, ...), custom_call_target="tpu_custom_call" | custom-call | tf_op jit(solution)/shard_map/sweep/pallas_call | solution.py:240
  46.9 2.3 %copy.10 = bf16[4,1,128,1024]{3,2,1,0:T(8,128)(2,1)} copy(bf16[4,1,128,1024]{3,2,1,0:T(8,128)(2,1)} %sweep.1) | data formatting | bytes 2097152

commit v3 on v2

--- a/solution.py
+++ b/solution.py
@@ -51,15 +51,18 @@
         def _(who=who):
             pl.semaphore_signal(barrier, inc=1, device_id=who, device_id_type=MESH)
 
-    loads = [pltpu.make_async_copy(inflow.at[0, :, q * W:(q + 1) * W], incs[0].at[q], ld.at[q]) for q in range(Q)]
-    loads += [
-        pltpu.make_async_copy(coup.at[0], coup_v, ld.at[Q]),
-        pltpu.make_async_copy(rhs.at[0, 0], rhs_v.at[0], ld.at[Q + 1]),
-        pltpu.make_async_copy(inv.at[0], inv_v, ld.at[Q + 2]),
-        pltpu.make_async_copy(off.at[0], off_v, ld.at[Q + 4]),
-        pltpu.make_async_copy(diag.at[0], diag_v, ld.at[Q + 3]),
+    first = [
+        pltpu.make_async_copy(inv.at[0], inv_v, ld.at[0]),
+        pltpu.make_async_copy(rhs.at[0, 0], rhs_v.at[0], ld.at[1]),
+        pltpu.make_async_copy(coup.at[0], coup_v, ld.at[2]),
     ]
-    loads += [pltpu.make_async_copy(rhs.at[t, 0], rhs_v.at[t], ld.at[Q + 4 + t]) for t in range(1, T)]
+    first += [pltpu.make_async_copy(inflow.at[0, :, q * W:(q + 1) * W], incs[0].at[q], ld.at[3 + q]) for q in range(Q)]
+    tiles = [
+        pltpu.make_async_copy(off.at[0], off_v, ld.at[3 + Q]),
+        pltpu.make_async_copy(diag.at[0], diag_v, ld.at[4 + Q]),
+    ]
+    later = [pltpu.make_async_copy(rhs.at[t, 0], rhs_v.at[t], ld.at[4 + Q + t]) for t in range(1, T)]
+    loads = first + tiles + later
     for c in loads:
         c.start()
 
@@ -139,10 +142,10 @@
         inc, rb, fa, fb = incs[t], rights[t], f0[t], f1[t]
         near0, other0, near1, other1 = copies(t)
         if t == 0:
-            for c in loads[:Q + 3]:
+            for c in first:
                 c.wait()
         else:
-            loads[Q + 4 + t].wait()
+            later[t - 1].wait()
 
             @pl.when(has_p)
             def _(t=t):
@@ -155,17 +158,18 @@
             x = x.astype(BF16)
             rb[r] = x
             fa[r + HALO] = mm(x, inv_v[r]).astype(BF16)
-            if n == 3:
-                if t == 0:
-                    pl.semaphore_wait(barrier, 1 + has_o.astype(jnp.int32) + has_p.astype(jnp.int32) + has_n.astype(jnp.int32))
+            if n == 3 and t > 0:
                 when_o(other0.start)
                 near0.start()
         if t == 0:
-            loads[Q + 3].wait()
+            for c in tiles:
+                c.wait()
             for r in order[:2]:
                 halo_operator(r)
+            pl.semaphore_wait(barrier, 1 + has_o.astype(jnp.int32) + has_p.astype(jnp.int32) + has_n.astype(jnp.int32))
+            near0.start()
+            when_o(other0.start)
             when_o(lambda: y_copy().start())
-            loads[Q + 4].wait()
         for r in order[:2]:
             part[r] = own(fa, rb, r)
         near0.wait_recv()
@@ -262,10 +266,10 @@
         + [pltpu.VMEM((N, M, W), BF16)] * T
         + [pltpu.VMEM((N + 2 * HALO, M, W), BF16)] * (2 * T)
         + [pltpu.VMEM((HALO, M, W), BF16)] * (4 * T)
-        + [DMA((Q + 4 + T,)), DMA((T,)), DMA((2 * T, 2)), DMA((2 * T, 2)), DMA((2,)), DMA((T - 1,)), DMA((T - 1,))],
-        compiler_params=pltpu.CompilerParams(collective_id=0, has_side_effects=True, vmem_limit_bytes=64000000),
+        + [DMA((4 + Q + T,)), DMA((T,)), DMA((2 * T, 2)), DMA((2 * T, 2)), DMA((2,)), DMA((T - 1,)), DMA((T - 1,))],
+        compiler_params=pltpu.CompilerParams(collective_id=0, has_side_effects=True, vmem_limit_bytes=48000000),
         name="sweep",
-    )(cols[0].T, iface, rhs, inflow, diag, off, inv, coup)
+    )(*[pltpu.with_memory_space_constraint(x, pltpu.HBM) for x in (cols[0].T, iface, rhs, inflow, diag, off, inv, coup)])
 
 
 def solution(mesh):

time: 49.3 us -> 47.3 us (0.959)
  the two profiles are of different devices: /device:TPU:391 before, /device:TPU:423 now
where the time goes in v3:
time: 47.3 us; the launch traced here: 47.1 us
  Pallas kernels  46.2 us (98%)
  local copies, waits for them, and re-layouts  0.97 us (2%)
    pallas_call x1, Pallas kernels, on_device(): pl.pallas_call(functools.partial(kernel, S, FN, T, N, K, Q, W), out_shape...  46.2 us
    unnamed x1, local copies, waits for them, and re-layouts  0.97 us

profile of v3, /device:TPU:423, one launch (start us, length us, event | category | flops | bytes accessed | tf_op | source)
XLA Modules:
  0.0 47.1 jit_solution(15905272600247726970)
XLA Ops:
  0.0 46.2 %sweep.1 = bf16[4,1,128,1024]{3,2,1,0:T(8,128)(2,1)S(1)} custom-call(s32[4,8]{1,0:T(4,128)} %bitcast.3, s32[2]{0:T(128)} %refs_1_.1, bf16[4,1,128,1024]{3,2,1,0:T(8,128)(2,1)} %refs_2_.1, bf16[1,128,256]{2,1,0:T(8,128)(2,1)} %refs_3_.1, bf16[1,8,128,128]{3,2,1,0:T(8,128)(2,1)} %refs_4_.1, bf16[1,8,4,128,128]{4,3,2,1,0:T(8,128)(2,1)} %refs_5_.1, ...), custom_call_target="tpu_custom_call" | custom-call | tf_op jit(solution)/shard_map/sweep/pallas_call | solution.py:244
  46.2 1.0 %copy.10 = bf16[4,1,128,1024]{3,2,1,0:T(8,128)(2,1)} copy(bf16[4,1,128,1024]{3,2,1,0:T(8,128)(2,1)S(1)} %sweep.1) | data formatting | bytes 2097152

commit v4 on v3

--- a/solution.py
+++ b/solution.py
@@ -8,6 +8,7 @@
 from jax.sharding import PartitionSpec as P
 
 HALO = 2
+DIAGONAL_FROM = 1
 MESH = pl.DeviceIdType.MESH
 BF16 = jnp.bfloat16
 F32 = jnp.float32
@@ -24,11 +25,12 @@
     (out,) = take(1)
     rhs_v, diag_v, off_v, inv_v, coup_v, out_v, sent = take(7)
     z, part, ypart, h1send, y_in = take(5)
+    fp, p_send, p_near, p_near_in, d_near, d_near_in, e0, e0_in, e1, e1_in, dinc = take(11)
     incs = take(T)
     rights = take(T)
     f0, f1 = take(T), take(T)
     n0, o0, n1, o1 = take(T), take(T), take(T), take(T)
-    ld, st, hs, hr, ysem, ssem, rsem = take(7)
+    ld, st, hs, hr, ysem, ssem, rsem, es, ps, ds, dr = take(11)
 
     s = lax.axis_index("slab")
     f = lax.axis_index("face")
@@ -39,6 +41,13 @@
     other = (s, jnp.clip(f - 1 + 2 * odd, 0, FN - 1))
     prev = (jnp.maximum(s - 1, 0), f)
     nxt = (jnp.minimum(s + 1, S - 1), f)
+    SE = FN // 2
+    seam = (f == SE - 1) | (f == SE)
+    duo = (f >= SE - 2) & (f <= SE + 1)
+    mate = duo & jnp.logical_not(seam)
+    plain_o = has_o & jnp.logical_not(seam)
+    across = jnp.where(f < SE, SE, SE - 1)
+    slot = jnp.where(seam, 0, 1)
     oe = odd * (N - HALO)
     ne = (N - HALO) - oe
     o_slot = odd * (N + HALO)
@@ -46,7 +55,8 @@
 
     barrier = pltpu.get_barrier_semaphore()
     pl.semaphore_signal(barrier, inc=1, device_id=near, device_id_type=MESH)
-    for there, who in ((has_o, other), (has_p, prev), (has_n, nxt)):
+    greeted = ((has_o, other), (has_p, prev), (has_n, nxt), (duo & has_n, (nxt[0], across)), (seam & has_p, (prev[0], across)), (seam & has_p, (prev[0], jnp.where(f < SE, SE + 1, SE - 2))))
+    for there, who in greeted:
         @pl.when(there)
         def _(who=who):
             pl.semaphore_signal(barrier, inc=1, device_id=who, device_id_type=MESH)
@@ -74,7 +84,7 @@
     e = [iface[q] for q in range(Q)]
 
     zero_halo = jnp.zeros((HALO,) + f0[0].shape[1:], BF16)
-    for b in f0 + f1:
+    for b in f0 + f1 + [fp]:
         b[0:HALO] = zero_halo
         b[N + HALO:N + 2 * HALO] = zero_halo
 
@@ -88,6 +98,10 @@
     def _():
         for b in incs[1:]:
             b[...] = jnp.zeros(b.shape, BF16)
+
+    @pl.when((s == 0) & seam)
+    def _():
+        dinc[...] = jnp.zeros(dinc.shape, BF16)
 
     def to_near(i, src, dst):
         return pltpu.make_async_remote_copy(src_ref=src, dst_ref=dst, send_sem=hs.at[i, 0], recv_sem=hr.at[i, 0], device_id=near, device_id_type=MESH)
@@ -110,15 +124,24 @@
     def forward(t):
         return pltpu.make_async_remote_copy(src_ref=sent.at[t], dst_ref=incs[t + 1], send_sem=ssem.at[t], recv_sem=rsem.at[t], device_id=nxt, device_id_type=MESH)
 
+    def diagonal(t, i):
+        return pltpu.make_async_remote_copy(src_ref=sent.at[t], dst_ref=dinc.at[t, i], send_sem=ds.at[t], recv_sem=dr.at[t, i], device_id=(nxt[0], across), device_id_type=MESH)
+
+    def swap(src, dst, sems, i, dev):
+        return pltpu.make_async_remote_copy(src_ref=src, dst_ref=dst, send_sem=sems.at[2 * i], recv_sem=sems.at[2 * i + 1], device_id=dev, device_id_type=MESH)
+
+    e_copies = [swap(e0, e0_in, es, 0, other), swap(e1, e1_in, es, 1, other)]
+    mate_copies = [swap(d_near, d_near_in, ps, 0, near), swap(p_near, p_near_in, ps, 1, near)]
+
     def when_o(act):
         @pl.when(has_o)
         def _():
             act()
 
-    def own(b, right_b, r):
+    def own(b, right_r, r):
         u = jnp.concatenate([b[r + HALO]] + [b[col(r, k)] for k in range(K)], axis=1)
         w = jnp.concatenate([diag_v[r]] + [off_v[r, k] for k in range(K)], axis=1)
-        corr = (right_b[r].astype(F32) - mm(u, w)).astype(BF16)
+        corr = (right_r.astype(F32) - mm(u, w)).astype(BF16)
         return b[r + HALO].astype(F32) + mm(corr, inv_v[r])
 
     def halo_operator(r):
@@ -136,72 +159,165 @@
         return jnp.concatenate([b[0], b[1]], axis=1)
 
     ZN, ZO = slice(0, HALO * W), slice(HALO * W, 2 * HALO * W)
+
+    def nn(a, b):
+        return jnp.dot(a, b, preferred_element_type=F32)
+
+    def rhs_row(t, r):
+        return rhs_v[t, :, pl.ds(pl.multiple_of(r * W, W), W)]
+
+    d = []
+
+    def placed(r):
+        return jnp.concatenate([jnp.where(e[q] == r, d[q].astype(F32), 0.0) for q in range(Q)], axis=1)
+
+    def mate_setup():
+        d.extend(nn(inv_v[e[q]], coup_v[q]).astype(BF16) for q in range(Q))
+
+        @pl.when(mate)
+        def _():
+            for j in range(HALO):
+                d_near[j] = placed(ne + j).astype(BF16)
+            mate_copies[0].start()
+            for t in range(1, T):
+                later[t - 1].wait()
+                for j in range(HALO):
+                    p_near[t - 1, j] = mm(rhs_row(t, ne + j), inv_v[ne + j]).astype(BF16)
+            mate_copies[1].start()
+
+        @pl.when(jnp.logical_not(mate))
+        def _():
+            for c in later:
+                c.wait()
+
+    def seam_operators():
+        @pl.when(seam)
+        def _():
+            mate_copies[0].wait_recv()
+            below = jnp.concatenate([d_near_in[j] for j in range(HALO)], axis=0)
+            for i in range(HALO):
+                r = oe + i
+                cs = [col(r, k) for k in range(K)]
+                at = []
+                for q in range(Q):
+                    x = jnp.where(e[q] == r, diag_v[r].astype(F32), 0.0)
+                    for k in range(K):
+                        x = x + jnp.where(cs[k] == e[q] + HALO, off_v[r, k].astype(F32), 0.0)
+                    at.append(x.astype(BF16))
+                y = nn(inv_v[r], jnp.concatenate(at, axis=1)).astype(BF16)
+                d_r = placed(r)
+                e0[i] = d_r.astype(BF16)
+                mine = jnp.concatenate([nn(y[:, q * W:(q + 1) * W], d[q]) for q in range(Q)], axis=1)
+                e1[i, :, 0:Q * W] = (2.0 * d_r - mine).astype(BF16)
+                e1[i, :, Q * W:2 * Q * W] = (-nn(z[r, :, ZN], below)).astype(BF16)
+            for c in e_copies:
+                c.start()
+
+    def seam_rows(t):
+        @pl.when(seam)
+        def _():
+            if t == DIAGONAL_FROM:
+                mate_copies[1].wait_recv()
+            for r in range(N):
+                fp[r + HALO] = mm(rhs_row(t, r), inv_v[r]).astype(BF16)
+            hn = jnp.concatenate([p_near_in[t - 1, j] for j in range(HALO)], axis=1)
+            for i in range(HALO):
+                p_send[t - 1, 0, i] = fp[oe + HALO + i]
+                p_send[t - 1, 1, i] = (own(fp, rhs_row(t, oe + i), oe + i) - mm(hn, z[oe + i, :, ZN])).astype(BF16)
+            to_other(2 * t, p_send.at[t - 1, 0], o0[t]).start()
+            to_other(2 * t + 1, p_send.at[t - 1, 1], o1[t]).start()
+
+    def complete(t, b, op, n):
+        vals = jnp.concatenate([dinc[t - 1, i, q] for i in range(n) for q in range(Q)], axis=1)
+        for j in range(HALO):
+            b[j] = (b[j].astype(F32) - mm(vals, op[j])).astype(BF16)
     order = [oe, oe + 1, ne, ne + 1] + list(range(HALO, N - HALO))
     stores = []
     for t in range(T):
         inc, rb, fa, fb = incs[t], rights[t], f0[t], f1[t]
         near0, other0, near1, other1 = copies(t)
+        crossing = has_o if t < DIAGONAL_FROM else plain_o
         if t == 0:
             for c in first:
                 c.wait()
         else:
-            later[t - 1].wait()
-
             @pl.when(has_p)
             def _(t=t):
                 forward(t - 1).wait_recv()
         coupled = [mm(inc[q], coup_v[q]) for q in range(Q)]
         for n, r in enumerate(order):
-            x = rhs_v[t, :, pl.ds(pl.multiple_of(r * W, W), W)].astype(F32)
+            x = rhs_row(t, r).astype(F32)
             for q in range(Q):
                 x = x - jnp.where(e[q] == r, coupled[q], 0.0)
             x = x.astype(BF16)
             rb[r] = x
             fa[r + HALO] = mm(x, inv_v[r]).astype(BF16)
             if n == 3 and t > 0:
-                when_o(other0.start)
+                pl.when(crossing)(other0.start)
                 near0.start()
         if t == 0:
             for c in tiles:
                 c.wait()
             for r in order[:2]:
                 halo_operator(r)
-            pl.semaphore_wait(barrier, 1 + has_o.astype(jnp.int32) + has_p.astype(jnp.int32) + has_n.astype(jnp.int32))
+            pl.semaphore_wait(barrier, 1 + sum(there.astype(jnp.int32) for there, _ in greeted))
             near0.start()
             when_o(other0.start)
             when_o(lambda: y_copy().start())
         for r in order[:2]:
-            part[r] = own(fa, rb, r)
+            part[r] = own(fa, rb[r], r)
         near0.wait_recv()
         hn = pair(n0[t])
         for i, r in enumerate(order[:2]):
             x = part[r] - mm(hn, z[r, :, ZN])
             part[r] = x
             h1send[t, i] = x.astype(BF16)
-        when_o(other1.start)
+        pl.when(crossing)(other1.start)
+        if t == 0:
+            mate_setup()
+        if DIAGONAL_FROM <= t + 1 < T:
+            seam_rows(t + 1)
+        if t == 0:
+            seam_operators()
         for r in order[2:]:
             if t == 0:
                 halo_operator(r)
-            part[r] = own(fa, rb, r) - mm(hn, z[r, :, ZN])
+            part[r] = own(fa, rb[r], r) - mm(hn, z[r, :, ZN])
         if t == 0:
             when_o(lambda: y_copy().wait_recv())
         mine = jnp.concatenate([fa[oe + HALO], fa[oe + HALO + 1]], axis=1)
         for i in range(HALO):
             ypart[i] = mm(mine, y_in[i])
         when_o(other0.wait_recv)
+        if t >= DIAGONAL_FROM:
+            @pl.when(seam)
+            def _(t=t):
+                if t == DIAGONAL_FROM:
+                    for c in e_copies:
+                        c.wait_recv()
+
+                @pl.when(has_p)
+                def _():
+                    for i in range(2):
+                        diagonal(t - 1, i).wait_recv()
+                complete(t, o0[t], e0_in, 1)
         ho = pair(o0[t])
         for n, r in enumerate(order[2:4] + order[:2] + order[4:]):
             fb[r + HALO] = (part[r] - mm(ho, z[r, :, ZO])).astype(BF16)
             if n == 1:
                 near1.start()
         if t + 1 < T:
-            mid = [own(fb, rb, e[q]) for q in range(Q)]
+            mid = [own(fb, rb[e[q]], e[q]) for q in range(Q)]
         else:
             mid = []
             for r in range(N):
-                part[r] = own(fb, rb, r)
+                part[r] = own(fb, rb[r], r)
+        when_o(other1.wait_recv)
+        if t >= DIAGONAL_FROM:
+            @pl.when(seam)
+            def _(t=t):
+                complete(t, o1[t], e1_in, 2)
         near1.wait_recv()
-        when_o(other1.wait_recv)
         far = [(o1[t][i].astype(F32) - ypart[i]).astype(BF16) for i in range(HALO)]
         both = jnp.concatenate([n1[t][0], n1[t][1]] + far, axis=1)
         if t + 1 < T:
@@ -211,8 +327,13 @@
             @pl.when(has_n)
             def _(t=t):
                 forward(t).start()
+
+            if t + 1 >= DIAGONAL_FROM:
+                @pl.when(has_n & duo)
+                def _(t=t):
+                    diagonal(t, slot).start()
             for r in range(N):
-                part[r] = own(fb, rb, r)
+                part[r] = own(fb, rb[r], r)
         for r in range(N):
             out_v[t, :, r * W:(r + 1) * W] = (part[r] - mm(both, z[r])).astype(BF16)
         c = pltpu.make_async_copy(out_v.at[t], out.at[t, 0], st.at[t])
@@ -230,6 +351,21 @@
         @pl.when(has_n)
         def _(t=t):
             forward(t).wait_send()
+
+        if t + 1 >= DIAGONAL_FROM:
+            @pl.when(has_n & duo)
+            def _(t=t):
+                diagonal(t, slot).wait_send()
+
+    @pl.when(seam)
+    def _():
+        for c in e_copies:
+            c.wait_send()
+
+    @pl.when(mate)
+    def _():
+        for c in mate_copies:
+            c.wait_send()
     for c in stores:
         c.wait()
 
@@ -261,12 +397,23 @@
             pltpu.VMEM((HALO, M, W), F32),
             pltpu.VMEM((T, HALO, M, W), BF16),
             pltpu.VMEM((HALO, W, HALO * W), BF16),
+            pltpu.VMEM((N + 2 * HALO, M, W), BF16),
+            pltpu.VMEM((T - 1, 2, HALO, M, W), BF16),
+            pltpu.VMEM((T - 1, HALO, M, W), BF16),
+            pltpu.VMEM((T - 1, HALO, M, W), BF16),
+            pltpu.VMEM((HALO, W, Q * W), BF16),
+            pltpu.VMEM((HALO, W, Q * W), BF16),
+            pltpu.VMEM((HALO, W, Q * W), BF16),
+            pltpu.VMEM((HALO, W, Q * W), BF16),
+            pltpu.VMEM((HALO, W, 2 * Q * W), BF16),
+            pltpu.VMEM((HALO, W, 2 * Q * W), BF16),
+            pltpu.VMEM((T - 1, 2, Q, M, W), BF16),
         ]
         + [pltpu.VMEM((Q, M, W), BF16)] * T
         + [pltpu.VMEM((N, M, W), BF16)] * T
         + [pltpu.VMEM((N + 2 * HALO, M, W), BF16)] * (2 * T)
         + [pltpu.VMEM((HALO, M, W), BF16)] * (4 * T)
-        + [DMA((4 + Q + T,)), DMA((T,)), DMA((2 * T, 2)), DMA((2 * T, 2)), DMA((2,)), DMA((T - 1,)), DMA((T - 1,))],
+        + [DMA((4 + Q + T,)), DMA((T,)), DMA((2 * T, 2)), DMA((2 * T, 2)), DMA((2,)), DMA((T - 1,)), DMA((T - 1,)), DMA((4,)), DMA((4,)), DMA((T - 1,)), DMA((T - 1, 2))],
         compiler_params=pltpu.CompilerParams(collective_id=0, has_side_effects=True, vmem_limit_bytes=48000000),
         name="sweep",
     )(*[pltpu.with_memory_space_constraint(x, pltpu.HBM) for x in (cols[0].T, iface, rhs, inflow, diag, off, inv, coup)])

time: 47.3 us -> 44.2 us (0.934)
  the two profiles are of different devices: /device:TPU:423 before, /device:TPU:421 now
where the time goes in v4:
time: 44.2 us; the launch traced here: 44 us
  Pallas kernels  43.1 us (98%)
  local copies, waits for them, and re-layouts  0.97 us (2%)
    pallas_call x1, Pallas kernels, on_device(): pl.pallas_call(functools.partial(kernel, S, FN, T, N, K, Q, W), out_shape...  43.1 us
    unnamed x1, local copies, waits for them, and re-layouts  0.97 us

profile of v4, /device:TPU:421, one launch (start us, length us, event | category | flops | bytes accessed | tf_op | source)
XLA Modules:
  0.0 44.0 jit_solution(2502812287271320612)
XLA Ops:
  0.0 43.1 %sweep.1 = bf16[4,1,128,1024]{3,2,1,0:T(8,128)(2,1)S(1)} custom-call(s32[4,8]{1,0:T(4,128)} %bitcast.3, s32[2]{0:T(128)} %refs_1_.1, bf16[4,1,128,1024]{3,2,1,0:T(8,128)(2,1)} %refs_2_.1, bf16[1,128,256]{2,1,0:T(8,128)(2,1)} %refs_3_.1, bf16[1,8,128,128]{3,2,1,0:T(8,128)(2,1)} %refs_4_.1, bf16[1,8,4,128,128]{4,3,2,1,0:T(8,128)(2,1)} %refs_5_.1, ...), custom_call_target="tpu_custom_call" | custom-call | tf_op jit(solution)/shard_map/sweep/pallas_call | solution.py:380
  43.1 1.0 %copy.10 = bf16[4,1,128,1024]{3,2,1,0:T(8,128)(2,1)} copy(bf16[4,1,128,1024]{3,2,1,0:T(8,128)(2,1)S(1)} %sweep.1) | data formatting | bytes 2097152

commit v5 on v4

--- a/solution.py
+++ b/solution.py
@@ -24,10 +24,9 @@
     cols, iface, rhs, inflow, diag, off, inv, coup = take(8)
     (out,) = take(1)
     rhs_v, diag_v, off_v, inv_v, coup_v, out_v, sent = take(7)
-    z, part, ypart, h1send, y_in = take(5)
+    z, part, ypart, h1send, y_in, g = take(6)
     fp, p_send, p_near, p_near_in, d_near, d_near_in, e0, e0_in, e1, e1_in, dinc = take(11)
     incs = take(T)
-    rights = take(T)
     f0, f1 = take(T), take(T)
     n0, o0, n1, o1 = take(T), take(T), take(T), take(T)
     ld, st, hs, hr, ysem, ssem, rsem, es, ps, ds, dr = take(11)
@@ -81,8 +80,6 @@
     def col(r, k):
         return jnp.clip(cols[k, r] - base, 0, N + 2 * HALO - 1)
 
-    e = [iface[q] for q in range(Q)]
-
     zero_halo = jnp.zeros((HALO,) + f0[0].shape[1:], BF16)
     for b in f0 + f1 + [fp]:
         b[0:HALO] = zero_halo
@@ -102,6 +99,8 @@
     @pl.when((s == 0) & seam)
     def _():
         dinc[...] = jnp.zeros(dinc.shape, BF16)
+
+    e = [iface[q] for q in range(Q)]
 
     def to_near(i, src, dst):
         return pltpu.make_async_remote_copy(src_ref=src, dst_ref=dst, send_sem=hs.at[i, 0], recv_sem=hr.at[i, 0], device_id=near, device_id_type=MESH)
@@ -119,7 +118,7 @@
         )
 
     def y_copy():
-        return pltpu.make_async_remote_copy(src_ref=z.at[pl.ds(oe, HALO), :, HALO * W:2 * HALO * W], dst_ref=y_in, send_sem=ysem.at[0], recv_sem=ysem.at[1], device_id=other, device_id_type=MESH)
+        return pltpu.make_async_remote_copy(src_ref=z.at[pl.ds(oe, HALO), :, (N + HALO) * W:(N + 2 * HALO) * W], dst_ref=y_in, send_sem=ysem.at[0], recv_sem=ysem.at[1], device_id=other, device_id_type=MESH)
 
     def forward(t):
         return pltpu.make_async_remote_copy(src_ref=sent.at[t], dst_ref=incs[t + 1], send_sem=ssem.at[t], recv_sem=rsem.at[t], device_id=nxt, device_id_type=MESH)
@@ -138,30 +137,43 @@
         def _():
             act()
 
-    def own(b, right_r, r):
-        u = jnp.concatenate([b[r + HALO]] + [b[col(r, k)] for k in range(K)], axis=1)
-        w = jnp.concatenate([diag_v[r]] + [off_v[r, k] for k in range(K)], axis=1)
-        corr = (right_r.astype(F32) - mm(u, w)).astype(BF16)
-        return b[r + HALO].astype(F32) + mm(corr, inv_v[r])
-
-    def halo_operator(r):
-        tiles = [off_v[r, k].astype(F32) for k in range(K)]
-        cs = [col(r, k) for k in range(K)]
-        sums = []
-        for slot in [n_slot + j for j in range(HALO)] + [o_slot + j for j in range(HALO)]:
-            x = jnp.zeros((W, W), F32)
-            for k in range(K):
-                x = x + jnp.where(cs[k] == slot, tiles[k], 0.0)
-            sums.append(x.astype(BF16))
-        z[r] = jnp.dot(inv_v[r], jnp.concatenate(sums, axis=1), preferred_element_type=F32).astype(BF16)
+    def operator_rows(r):
+        prod = jnp.dot(inv_v[r], jnp.concatenate([diag_v[r]] + [off_v[r, k] for k in range(K)], axis=1), preferred_element_type=F32)
+        prod = prod.astype(BF16)
+        tiles = [prod[:, k * W:(k + 1) * W] for k in range(K + 1)]
+        cs = [r + HALO] + [col(r, k) for k in range(K)]
+        slots = [c + HALO for c in range(N)] + [n_slot + j for j in range(HALO)] + [o_slot + j for j in range(HALO)]
+        for c, slot in enumerate(slots):
+            x = None
+            for k in range(0 if c < N else 1, K + 1):
+                y = jnp.where(cs[k] == slot, tiles[k], jnp.zeros((), BF16))
+                x = y if x is None else x + y
+            z[r, :, c * W:(c + 1) * W] = x
+
+    def block_of(b):
+        return jnp.concatenate([b[c + HALO] for c in range(N)], axis=1)
+
+    OWN, ZN, ZO = slice(0, N * W), slice(N * W, (N + HALO) * W), slice((N + HALO) * W, (N + 2 * HALO) * W)
+    HALOS = slice(N * W, (N + 2 * HALO) * W)
+
+    def own(b, p):
+        return [b[p + i + HALO].astype(F32) + g[p + i] - x for i, x in enumerate(halo_term(block_of(b), p, OWN))]
+
+    def rows_of(p, q, part_of):
+        return jnp.concatenate([z[p, :, part_of], z[q, :, part_of]], axis=0)
+
+    def halo_term(v, p, part_of):
+        x = mm(v, z[pl.ds(p, 2), :, part_of].reshape(2 * W, v.shape[1]))
+        return x[:, :W], x[:, W:]
 
     def pair(b):
         return jnp.concatenate([b[0], b[1]], axis=1)
 
-    ZN, ZO = slice(0, HALO * W), slice(HALO * W, 2 * HALO * W)
 
     def nn(a, b):
         return jnp.dot(a, b, preferred_element_type=F32)
+
+    order = [oe, oe + 1, ne, ne + 1] + list(range(HALO, N - HALO))
 
     def rhs_row(t, r):
         return rhs_v[t, :, pl.ds(pl.multiple_of(r * W, W), W)]
@@ -190,6 +202,12 @@
             for c in later:
                 c.wait()
 
+    def own_tile(r, c):
+        x = jnp.zeros((W, W), BF16)
+        for j in range(N):
+            x = x + jnp.where(c == j, z[r, :, j * W:(j + 1) * W], jnp.zeros((), BF16))
+        return x
+
     def seam_operators():
         @pl.when(seam)
         def _():
@@ -197,17 +215,9 @@
             below = jnp.concatenate([d_near_in[j] for j in range(HALO)], axis=0)
             for i in range(HALO):
                 r = oe + i
-                cs = [col(r, k) for k in range(K)]
-                at = []
-                for q in range(Q):
-                    x = jnp.where(e[q] == r, diag_v[r].astype(F32), 0.0)
-                    for k in range(K):
-                        x = x + jnp.where(cs[k] == e[q] + HALO, off_v[r, k].astype(F32), 0.0)
-                    at.append(x.astype(BF16))
-                y = nn(inv_v[r], jnp.concatenate(at, axis=1)).astype(BF16)
                 d_r = placed(r)
                 e0[i] = d_r.astype(BF16)
-                mine = jnp.concatenate([nn(y[:, q * W:(q + 1) * W], d[q]) for q in range(Q)], axis=1)
+                mine = jnp.concatenate([nn(own_tile(r, e[q]), d[q]) for q in range(Q)], axis=1)
                 e1[i, :, 0:Q * W] = (2.0 * d_r - mine).astype(BF16)
                 e1[i, :, Q * W:2 * Q * W] = (-nn(z[r, :, ZN], below)).astype(BF16)
             for c in e_copies:
@@ -218,12 +228,16 @@
         def _():
             if t == DIAGONAL_FROM:
                 mate_copies[1].wait_recv()
-            for r in range(N):
-                fp[r + HALO] = mm(rhs_row(t, r), inv_v[r]).astype(BF16)
+            edge = []
+            for r in order:
+                x = mm(rhs_row(t, r), inv_v[r])
+                fp[r + HALO] = x.astype(BF16)
+                if len(edge) < HALO:
+                    edge.append(x)
             hn = jnp.concatenate([p_near_in[t - 1, j] for j in range(HALO)], axis=1)
-            for i in range(HALO):
+            for i, (x, y) in enumerate(zip(halo_term(block_of(fp), oe, OWN), halo_term(hn, oe, ZN))):
                 p_send[t - 1, 0, i] = fp[oe + HALO + i]
-                p_send[t - 1, 1, i] = (own(fp, rhs_row(t, oe + i), oe + i) - mm(hn, z[oe + i, :, ZN])).astype(BF16)
+                p_send[t - 1, 1, i] = (fp[oe + HALO + i].astype(F32) + edge[i] - x - y).astype(BF16)
             to_other(2 * t, p_send.at[t - 1, 0], o0[t]).start()
             to_other(2 * t + 1, p_send.at[t - 1, 1], o1[t]).start()
 
@@ -231,10 +245,9 @@
         vals = jnp.concatenate([dinc[t - 1, i, q] for i in range(n) for q in range(Q)], axis=1)
         for j in range(HALO):
             b[j] = (b[j].astype(F32) - mm(vals, op[j])).astype(BF16)
-    order = [oe, oe + 1, ne, ne + 1] + list(range(HALO, N - HALO))
     stores = []
     for t in range(T):
-        inc, rb, fa, fb = incs[t], rights[t], f0[t], f1[t]
+        inc, fa, fb = incs[t], f0[t], f1[t]
         near0, other0, near1, other1 = copies(t)
         crossing = has_o if t < DIAGONAL_FROM else plain_o
         if t == 0:
@@ -249,9 +262,9 @@
             x = rhs_row(t, r).astype(F32)
             for q in range(Q):
                 x = x - jnp.where(e[q] == r, coupled[q], 0.0)
-            x = x.astype(BF16)
-            rb[r] = x
-            fa[r + HALO] = mm(x, inv_v[r]).astype(BF16)
+            x = mm(x.astype(BF16), inv_v[r])
+            g[r] = x
+            fa[r + HALO] = x.astype(BF16)
             if n == 3 and t > 0:
                 pl.when(crossing)(other0.start)
                 near0.start()
@@ -259,18 +272,18 @@
             for c in tiles:
                 c.wait()
             for r in order[:2]:
-                halo_operator(r)
+                operator_rows(r)
             pl.semaphore_wait(barrier, 1 + sum(there.astype(jnp.int32) for there, _ in greeted))
             near0.start()
             when_o(other0.start)
             when_o(lambda: y_copy().start())
-        for r in order[:2]:
-            part[r] = own(fa, rb[r], r)
+        for i, x in enumerate(own(fa, oe)):
+            part[oe + i] = x
         near0.wait_recv()
         hn = pair(n0[t])
-        for i, r in enumerate(order[:2]):
-            x = part[r] - mm(hn, z[r, :, ZN])
-            part[r] = x
+        for i, x in enumerate(halo_term(hn, oe, ZN)):
+            x = part[oe + i] - x
+            part[oe + i] = x
             h1send[t, i] = x.astype(BF16)
         pl.when(crossing)(other1.start)
         if t == 0:
@@ -279,10 +292,12 @@
             seam_rows(t + 1)
         if t == 0:
             seam_operators()
-        for r in order[2:]:
+        for p in order[2::2]:
             if t == 0:
-                halo_operator(r)
-            part[r] = own(fa, rb[r], r) - mm(hn, z[r, :, ZN])
+                operator_rows(p)
+                operator_rows(p + 1)
+            for i, (x, y) in enumerate(zip(own(fa, p), halo_term(hn, p, ZN))):
+                part[p + i] = x - y
         if t == 0:
             when_o(lambda: y_copy().wait_recv())
         mine = jnp.concatenate([fa[oe + HALO], fa[oe + HALO + 1]], axis=1)
@@ -302,16 +317,18 @@
                         diagonal(t - 1, i).wait_recv()
                 complete(t, o0[t], e0_in, 1)
         ho = pair(o0[t])
-        for n, r in enumerate(order[2:4] + order[:2] + order[4:]):
-            fb[r + HALO] = (part[r] - mm(ho, z[r, :, ZO])).astype(BF16)
-            if n == 1:
+        for n, p in enumerate([ne, oe] + order[4::2]):
+            for i, x in enumerate(halo_term(ho, p, ZO)):
+                fb[p + i + HALO] = (part[p + i] - x).astype(BF16)
+            if n == 0:
                 near1.start()
         if t + 1 < T:
-            mid = [own(fb, rb[e[q]], e[q]) for q in range(Q)]
+            x = mm(block_of(fb), rows_of(e[0], e[1], OWN))
+            mid = [fb[e[q] + HALO].astype(F32) + g[e[q]] - x[:, q * W:(q + 1) * W] for q in range(Q)]
         else:
-            mid = []
-            for r in range(N):
-                part[r] = own(fb, rb[r], r)
+            for p in range(0, N, 2):
+                for i, x in enumerate(own(fb, p)):
+                    part[p + i] = x
         when_o(other1.wait_recv)
         if t >= DIAGONAL_FROM:
             @pl.when(seam)
@@ -321,8 +338,9 @@
         far = [(o1[t][i].astype(F32) - ypart[i]).astype(BF16) for i in range(HALO)]
         both = jnp.concatenate([n1[t][0], n1[t][1]] + far, axis=1)
         if t + 1 < T:
+            x = mm(both, rows_of(e[0], e[1], HALOS))
             for q in range(Q):
-                sent[t, q] = (mid[q] - mm(both, z[e[q]])).astype(BF16)
+                sent[t, q] = (mid[q] - x[:, q * W:(q + 1) * W]).astype(BF16)
 
             @pl.when(has_n)
             def _(t=t):
@@ -332,13 +350,17 @@
                 @pl.when(has_n & duo)
                 def _(t=t):
                     diagonal(t, slot).start()
-            for r in range(N):
-                part[r] = own(fb, rb[r], r)
-        for r in range(N):
-            out_v[t, :, r * W:(r + 1) * W] = (part[r] - mm(both, z[r])).astype(BF16)
-        c = pltpu.make_async_copy(out_v.at[t], out.at[t, 0], st.at[t])
-        c.start()
-        stores.append(c)
+            for p in range(0, N, 2):
+                for i, x in enumerate(own(fb, p)):
+                    part[p + i] = x
+        for p in range(0, N, 2):
+            for i, x in enumerate(halo_term(both, p, HALOS)):
+                out_v[t, :, (p + i) * W:(p + i + 1) * W] = (part[p + i] - x).astype(BF16)
+            if p % 4 == 2:
+                cut = slice((p - 2) * W, (p + 2) * W)
+                c = pltpu.make_async_copy(out_v.at[t, :, cut], out.at[t, 0, :, cut], st.at[t, p // 4])
+                c.start()
+                stores.append(c)
 
     for t in range(T):
         near0, other0, near1, other1 = copies(t)
@@ -392,11 +414,12 @@
             pltpu.VMEM((T - 1, Q, M, W), BF16),
         ]
         + [
-            pltpu.VMEM((N, W, 2 * HALO * W), BF16),
+            pltpu.VMEM((N, W, (N + 2 * HALO) * W), BF16),
             pltpu.VMEM((N, M, W), F32),
             pltpu.VMEM((HALO, M, W), F32),
             pltpu.VMEM((T, HALO, M, W), BF16),
             pltpu.VMEM((HALO, W, HALO * W), BF16),
+            pltpu.VMEM((N, M, W), F32),
             pltpu.VMEM((N + 2 * HALO, M, W), BF16),
             pltpu.VMEM((T - 1, 2, HALO, M, W), BF16),
             pltpu.VMEM((T - 1, HALO, M, W), BF16),
@@ -410,10 +433,9 @@
             pltpu.VMEM((T - 1, 2, Q, M, W), BF16),
         ]
         + [pltpu.VMEM((Q, M, W), BF16)] * T
-        + [pltpu.VMEM((N, M, W), BF16)] * T
         + [pltpu.VMEM((N + 2 * HALO, M, W), BF16)] * (2 * T)
         + [pltpu.VMEM((HALO, M, W), BF16)] * (4 * T)
-        + [DMA((4 + Q + T,)), DMA((T,)), DMA((2 * T, 2)), DMA((2 * T, 2)), DMA((2,)), DMA((T - 1,)), DMA((T - 1,)), DMA((4,)), DMA((4,)), DMA((T - 1,)), DMA((T - 1, 2))],
+        + [DMA((4 + Q + T,)), DMA((T, N // 4)), DMA((2 * T, 2)), DMA((2 * T, 2)), DMA((2,)), DMA((T - 1,)), DMA((T - 1,)), DMA((4,)), DMA((4,)), DMA((T - 1,)), DMA((T - 1, 2))],
         compiler_params=pltpu.CompilerParams(collective_id=0, has_side_effects=True, vmem_limit_bytes=48000000),
         name="sweep",
     )(*[pltpu.with_memory_space_constraint(x, pltpu.HBM) for x in (cols[0].T, iface, rhs, inflow, diag, off, inv, coup)])

time: 44.2 us -> 43.8 us (level)
  the two profiles are of different devices: /device:TPU:421 before, /device:TPU:409 now
where the time goes in v5:
time: 43.8 us; the launch traced here: 43.7 us
  Pallas kernels  42.7 us (97%)
  local copies, waits for them, and re-layouts  0.97 us (2%)
    pallas_call x1, Pallas kernels, on_device(): pl.pallas_call(functools.partial(kernel, S, FN, T, N, K, Q, W), out_shape...  42.7 us
    unnamed x1, local copies, waits for them, and re-layouts  0.97 us

profile of v5, /device:TPU:409, one launch (start us, length us, event | category | flops | bytes accessed | tf_op | source)
XLA Modules:
  0.0 43.7 jit_solution(427453655388903542)
XLA Ops:
  0.0 42.7 %sweep.1 = bf16[4,1,128,1024]{3,2,1,0:T(8,128)(2,1)S(1)} custom-call(s32[4,8]{1,0:T(4,128)} %bitcast.3, s32[2]{0:T(128)} %refs_1_.1, bf16[4,1,128,1024]{3,2,1,0:T(8,128)(2,1)} %refs_2_.1, bf16[1,128,256]{2,1,0:T(8,128)(2,1)} %refs_3_.1, bf16[1,8,128,128]{3,2,1,0:T(8,128)(2,1)} %refs_4_.1, bf16[1,8,4,128,128]{4,3,2,1,0:T(8,128)(2,1)} %refs_5_.1, ...), custom_call_target="tpu_custom_call" | custom-call | tf_op jit(solution)/shard_map/sweep/pallas_call | solution.py:402
  42.7 1.0 %copy.10 = bf16[4,1,128,1024]{3,2,1,0:T(8,128)(2,1)} copy(bf16[4,1,128,1024]{3,2,1,0:T(8,128)(2,1)S(1)} %sweep.1) | data formatting | bytes 2097152

commit v6 on v5

--- a/solution.py
+++ b/solution.py
@@ -21,7 +21,7 @@
 def kernel(S, FN, T, N, K, Q, W, *refs):
     refs = list(refs)
     take = lambda n: [refs.pop(0) for _ in range(n)]
-    cols, iface, rhs, inflow, diag, off, inv, coup = take(8)
+    cols_h, iface_h, rhs, inflow, diag, off, inv, coup = take(8)
     (out,) = take(1)
     rhs_v, diag_v, off_v, inv_v, coup_v, out_v, sent = take(7)
     z, part, ypart, h1send, y_in, g = take(6)
@@ -29,7 +29,7 @@
     incs = take(T)
     f0, f1 = take(T), take(T)
     n0, o0, n1, o1 = take(T), take(T), take(T), take(T)
-    ld, st, hs, hr, ysem, ssem, rsem, es, ps, ds, dr = take(11)
+    ld, st, hs, hr, ysem, ssem, rsem, es, ps, ds, dr, cols, iface, ints = take(14)
 
     s = lax.axis_index("slab")
     f = lax.axis_index("face")
@@ -60,6 +60,7 @@
         def _(who=who):
             pl.semaphore_signal(barrier, inc=1, device_id=who, device_id_type=MESH)
 
+    index = [pltpu.make_async_copy(cols_h, cols, ints.at[0]), pltpu.make_async_copy(iface_h, iface, ints.at[1])]
     first = [
         pltpu.make_async_copy(inv.at[0], inv_v, ld.at[0]),
         pltpu.make_async_copy(rhs.at[0, 0], rhs_v.at[0], ld.at[1]),
@@ -71,7 +72,7 @@
         pltpu.make_async_copy(diag.at[0], diag_v, ld.at[4 + Q]),
     ]
     later = [pltpu.make_async_copy(rhs.at[t, 0], rhs_v.at[t], ld.at[4 + Q + t]) for t in range(1, T)]
-    loads = first + tiles + later
+    loads = index + first + tiles + later
     for c in loads:
         c.start()
 
@@ -100,6 +101,8 @@
     def _():
         dinc[...] = jnp.zeros(dinc.shape, BF16)
 
+    for c in index:
+        c.wait()
     e = [iface[q] for q in range(Q)]
 
     def to_near(i, src, dst):
@@ -265,7 +268,9 @@
             x = mm(x.astype(BF16), inv_v[r])
             g[r] = x
             fa[r + HALO] = x.astype(BF16)
-            if n == 3 and t > 0:
+            if n == 3:
+                if t == 0:
+                    pl.semaphore_wait(barrier, 1 + sum(there.astype(jnp.int32) for there, _ in greeted))
                 pl.when(crossing)(other0.start)
                 near0.start()
         if t == 0:
@@ -273,9 +278,6 @@
                 c.wait()
             for r in order[:2]:
                 operator_rows(r)
-            pl.semaphore_wait(barrier, 1 + sum(there.astype(jnp.int32) for there, _ in greeted))
-            near0.start()
-            when_o(other0.start)
             when_o(lambda: y_copy().start())
         for i, x in enumerate(own(fa, oe)):
             part[oe + i] = x
@@ -397,12 +399,11 @@
     _, N, K, W, _ = off.shape
     Q = coup.shape[1]
     ANY = pl.BlockSpec(memory_space=pl.ANY)
-    SM = pl.BlockSpec(memory_space=pltpu.SMEM)
     DMA = pltpu.SemaphoreType.DMA
     return pl.pallas_call(
         functools.partial(kernel, S, FN, T, N, K, Q, W),
         out_shape=jax.ShapeDtypeStruct(rhs.shape, BF16),
-        in_specs=[SM, SM] + [ANY] * 6,
+        in_specs=[ANY] * 8,
         out_specs=ANY,
         scratch_shapes=[
             pltpu.VMEM((T, M, N * W), BF16),
@@ -435,7 +436,7 @@
         + [pltpu.VMEM((Q, M, W), BF16)] * T
         + [pltpu.VMEM((N + 2 * HALO, M, W), BF16)] * (2 * T)
         + [pltpu.VMEM((HALO, M, W), BF16)] * (4 * T)
-        + [DMA((4 + Q + T,)), DMA((T, N // 4)), DMA((2 * T, 2)), DMA((2 * T, 2)), DMA((2,)), DMA((T - 1,)), DMA((T - 1,)), DMA((4,)), DMA((4,)), DMA((T - 1,)), DMA((T - 1, 2))],
+        + [DMA((4 + Q + T,)), DMA((T, N // 4)), DMA((2 * T, 2)), DMA((2 * T, 2)), DMA((2,)), DMA((T - 1,)), DMA((T - 1,)), DMA((4,)), DMA((4,)), DMA((T - 1,)), DMA((T - 1, 2)), pltpu.SMEM((K, N), jnp.int32), pltpu.SMEM((Q,), jnp.int32), DMA((2,))],
         compiler_params=pltpu.CompilerParams(collective_id=0, has_side_effects=True, vmem_limit_bytes=48000000),
         name="sweep",
     )(*[pltpu.with_memory_space_constraint(x, pltpu.HBM) for x in (cols[0].T, iface, rhs, inflow, diag, off, inv, coup)])

time: 43.8 us -> 42.9 us (0.979)
  Pallas kernels: 42.7 us -> 41.8 us
    pallas_call x1, Pallas kernels: 42.7 us -> 41.8 us  [on_device(): pl.pallas_call(functools.partial(kernel, S, FN, T, N, K, Q, W), out_shape...]
where the time goes in v6:
time: 42.9 us; the launch traced here: 42.7 us
  Pallas kernels  41.8 us (97%)
  local copies, waits for them, and re-layouts  0.97 us (2%)
    pallas_call x1, Pallas kernels, on_device(): pl.pallas_call(functools.partial(kernel, S, FN, T, N, K, Q, W), out_shape...  41.8 us
    unnamed x1, local copies, waits for them, and re-layouts  0.97 us

profile of v6, /device:TPU:409, one launch (start us, length us, event | category | flops | bytes accessed | tf_op | source)
XLA Modules:
  0.0 42.7 jit_solution(7521192189569774338)
XLA Ops:
  0.0 41.8 %sweep.1 = bf16[4,1,128,1024]{3,2,1,0:T(8,128)(2,1)S(1)} custom-call(s32[4,8]{1,0:T(4,128)} %bitcast.3, s32[2]{0:T(128)} %refs_1_.1, bf16[4,1,128,1024]{3,2,1,0:T(8,128)(2,1)} %refs_2_.1, bf16[1,128,256]{2,1,0:T(8,128)(2,1)} %refs_3_.1, bf16[1,8,128,128]{3,2,1,0:T(8,128)(2,1)} %refs_4_.1, bf16[1,8,4,128,128]{4,3,2,1,0:T(8,128)(2,1)} %refs_5_.1, ...), custom_call_target="tpu_custom_call" | custom-call | tf_op jit(solution)/shard_map/sweep/pallas_call | solution.py:403
  41.8 1.0 %copy.10 = bf16[4,1,128,1024]{3,2,1,0:T(8,128)(2,1)} copy(bf16[4,1,128,1024]{3,2,1,0:T(8,128)(2,1)S(1)} %sweep.1) | data formatting | bytes 2097152

commit v7 on v6

--- a/solution.py
+++ b/solution.py
@@ -103,7 +103,7 @@
 
     for c in index:
         c.wait()
-    e = [iface[q] for q in range(Q)]
+    e = [jnp.clip(iface[q], 0, N - 1) for q in range(Q)]
 
     def to_near(i, src, dst):
         return pltpu.make_async_remote_copy(src_ref=src, dst_ref=dst, send_sem=hs.at[i, 0], recv_sem=hr.at[i, 0], device_id=near, device_id_type=MESH)
@@ -268,10 +268,11 @@
             x = mm(x.astype(BF16), inv_v[r])
             g[r] = x
             fa[r + HALO] = x.astype(BF16)
-            if n == 3:
+            if n == (3 if t == 0 else 1):
                 if t == 0:
                     pl.semaphore_wait(barrier, 1 + sum(there.astype(jnp.int32) for there, _ in greeted))
                 pl.when(crossing)(other0.start)
+            if n == 3:
                 near0.start()
         if t == 0:
             for c in tiles:
@@ -281,6 +282,8 @@
             when_o(lambda: y_copy().start())
         for i, x in enumerate(own(fa, oe)):
             part[oe + i] = x
+        if t > 0 and DIAGONAL_FROM <= t + 1 < T:
+            seam_rows(t + 1)
         near0.wait_recv()
         hn = pair(n0[t])
         for i, x in enumerate(halo_term(hn, oe, ZN)):
@@ -290,9 +293,8 @@
         pl.when(crossing)(other1.start)
         if t == 0:
             mate_setup()
-        if DIAGONAL_FROM <= t + 1 < T:
-            seam_rows(t + 1)
-        if t == 0:
+            if DIAGONAL_FROM == 1:
+                seam_rows(1)
             seam_operators()
         for p in order[2::2]:
             if t == 0:
@@ -336,11 +338,19 @@
             @pl.when(seam)
             def _(t=t):
                 complete(t, o1[t], e1_in, 2)
+        far = [(o1[t][i].astype(F32) - ypart[i]).astype(BF16) for i in range(HALO)]
+        far = jnp.concatenate(far, axis=1)
+        if t + 1 < T:
+            x = mm(far, rows_of(e[0], e[1], ZO))
+            mid = [mid[q] - x[:, q * W:(q + 1) * W] for q in range(Q)]
+        else:
+            for p in range(0, N, 2):
+                for i, x in enumerate(halo_term(far, p, ZO)):
+                    part[p + i] = part[p + i] - x
         near1.wait_recv()
-        far = [(o1[t][i].astype(F32) - ypart[i]).astype(BF16) for i in range(HALO)]
-        both = jnp.concatenate([n1[t][0], n1[t][1]] + far, axis=1)
+        hn = pair(n1[t])
         if t + 1 < T:
-            x = mm(both, rows_of(e[0], e[1], HALOS))
+            x = mm(hn, rows_of(e[0], e[1], ZN))
             for q in range(Q):
                 sent[t, q] = (mid[q] - x[:, q * W:(q + 1) * W]).astype(BF16)
 
@@ -356,7 +366,9 @@
                 for i, x in enumerate(own(fb, p)):
                     part[p + i] = x
         for p in range(0, N, 2):
-            for i, x in enumerate(halo_term(both, p, HALOS)):
+            last = t + 1 == T
+            vals = hn if last else jnp.concatenate([hn, far], axis=1)
+            for i, x in enumerate(halo_term(vals, p, ZN if last else HALOS)):
                 out_v[t, :, (p + i) * W:(p + i + 1) * W] = (part[p + i] - x).astype(BF16)
             if p % 4 == 2:
                 cut = slice((p - 2) * W, (p + 2) * W)

time: 42.9 us -> 42.8 us (level)
  no operation moved by 1% of the time
where the time goes in v7:
time: 42.8 us; the launch traced here: 42.7 us
  Pallas kernels  41.7 us (97%)
  local copies, waits for them, and re-layouts  0.97 us (2%)
    pallas_call x1, Pallas kernels, on_device(): pl.pallas_call(functools.partial(kernel, S, FN, T, N, K, Q, W), out_shape...  41.7 us
    unnamed x1, local copies, waits for them, and re-layouts  0.97 us

profile of v7, /device:TPU:409, one launch (start us, length us, event | category | flops | bytes accessed | tf_op | source)
XLA Modules:
  0.0 42.7 jit_solution(2642095163989905555)
XLA Ops:
  0.0 41.7 %sweep.1 = bf16[4,1,128,1024]{3,2,1,0:T(8,128)(2,1)S(1)} custom-call(s32[4,8]{1,0:T(4,128)} %bitcast.3, s32[2]{0:T(128)} %refs_1_.1, bf16[4,1,128,1024]{3,2,1,0:T(8,128)(2,1)} %refs_2_.1, bf16[1,128,256]{2,1,0:T(8,128)(2,1)} %refs_3_.1, bf16[1,8,128,128]{3,2,1,0:T(8,128)(2,1)} %refs_4_.1, bf16[1,8,4,128,128]{4,3,2,1,0:T(8,128)(2,1)} %refs_5_.1, ...), custom_call_target="tpu_custom_call" | custom-call | tf_op jit(solution)/shard_map/sweep/pallas_call | solution.py:415
  41.7 1.0 %copy.10 = bf16[4,1,128,1024]{3,2,1,0:T(8,128)(2,1)} copy(bf16[4,1,128,1024]{3,2,1,0:T(8,128)(2,1)S(1)} %sweep.1) | data formatting | bytes 2097152
